TPU v7x, 32 devices: a whole 2x2x4 slice. The times are simulated.
32 devices in a mesh: grp: 4 (over x, core), seq: 8 (over z, y).
Axes of the slice: x: 2, y: 2, z: 4, core: 2. Of those that a mesh axis runs over, the one named last changes fastest.
Arguments:
- cand_queries: bfloat16 [4096, 128, 128], P(('grp', 'seq')), may hold values from -256 to 256
- candidate_keys: bfloat16 [512, 128, 128], P(('grp', 'seq')), may hold values from -6 to 6
- candidate_values: bfloat16 [512, 128, 128], P(('grp', 'seq')), may hold values from -24 to 24
- prefix_rotated_keys: bfloat16 [128, 1024], P(('grp', 'seq')), may hold values from -6.1 to 6.1
- prefix_value_matrix: bfloat16 [128, 1024], P(('grp', 'seq')), may hold values from -24 to 24
- lengths: int32 [64], replicated, may hold values from 32 to 128
Outputs:
- attended: bfloat16 [4096, 128, 128], P(('grp', 'seq'))
All inputs are finite; a program needn't handle non-finite values.
Results may differ from a plain program's by a relative error of at most 0.0076.
Values may be sent and summed in bfloat16 or wider, within the bound.
No kernel may reach another device: no remote copies, remote signals or barrier semaphores. Data moves between devices by JAX's collectives and lax.ppermute only.
A program may use at most 64 MiB of HBM per device.

v0:
```python
import math

import jax
import jax.numpy as jnp
import numpy as np
from jax import lax
from jax.sharding import PartitionSpec as P

QUERY_HEADS = 64
KEY_VALUE_HEADS = 8
HEAD_WIDTH = 128


rope_base = 500000.0


def rotate(vectors, positions):
    half_width = vectors.shape[-1] // 2
    exponents = jnp.arange(half_width, dtype=jnp.float32) * (2.0 / vectors.shape[-1])
    frequency = 1.0 / jnp.power(jnp.float32(rope_base), exponents)
    angles = positions.astype(jnp.float32)[:, None] * frequency[None, :]
    cosine = jnp.cos(angles)
    sine_table = jnp.sin(angles)
    lower_half = vectors[..., :half_width]
    upper_half = vectors[..., half_width:]
    return jnp.concatenate(
        [
            lower_half * cosine - upper_half * sine_table,
            upper_half * cosine + lower_half * sine_table,
        ],
        axis=-1,
    )


def pick_heads(key_row_list, value_row_list, head_table, sequence_count):
    row_total = key_row_list.shape[0]
    stacked = jnp.stack(
        [
            key_row_list.reshape(row_total, KEY_VALUE_HEADS, HEAD_WIDTH),
            value_row_list.reshape(row_total, KEY_VALUE_HEADS, HEAD_WIDTH),
        ],
        axis=2,
    )
    picked = jnp.take(stacked, head_table, axis=1)
    return picked.reshape(row_total, sequence_count, -1).transpose(1, 0, 2)


def shards(
    cand_queries,
    candidate_keys,
    candidate_values,
    prefix_rotated_keys,
    prefix_value_matrix,
    lengths,
):
    sequence_count = lax.axis_size("seq")
    grp_count = lax.axis_size("grp")
    head_rows = cand_queries.shape[0]
    cand_length = cand_queries.shape[1]
    key_value_rows = candidate_keys.shape[0]
    group_width = QUERY_HEADS // KEY_VALUE_HEADS
    key_value_heads = min(KEY_VALUE_HEADS, key_value_rows)
    prefix_here = prefix_rotated_keys.shape[0]
    prefix_total = prefix_here * sequence_count * grp_count
    score_scale = 1.0 / math.sqrt(HEAD_WIDTH)
    prefix_pick = (
        (np.arange(sequence_count)[:, None] * key_value_rows + np.arange(key_value_heads)[None, :])
        % KEY_VALUE_HEADS
    ).reshape(-1)
    outgoing = pick_heads(prefix_rotated_keys, prefix_value_matrix, prefix_pick, sequence_count)
    spread = lax.all_to_all(outgoing, "seq", split_axis=0, concat_axis=1, tiled=True)
    prefix_pair = lax.all_gather(spread, "grp", axis=1, tiled=True)
    prefix_pair = prefix_pair.reshape(prefix_total, key_value_heads, 2, HEAD_WIDTH)
    kv_table = np.arange(key_value_rows) % key_value_heads
    prefix_key_rows = jnp.take(prefix_pair[:, :, 0], kv_table, axis=1).transpose(1, 0, 2)
    prefix_value_rows = jnp.take(prefix_pair[:, :, 1], kv_table, axis=1).transpose(1, 0, 2)
    positions = prefix_total + jnp.arange(cand_length, dtype=jnp.int32)
    new_keys = rotate(candidate_keys.astype(jnp.float32), positions).astype(jnp.bfloat16)
    rotated = rotate(cand_queries.astype(jnp.float32), positions).astype(jnp.bfloat16)
    rotated = rotated.reshape(key_value_rows, group_width * cand_length, HEAD_WIDTH)
    all_keys = jnp.concatenate([prefix_key_rows, new_keys], axis=1)
    all_values = jnp.concatenate([prefix_value_rows, candidate_values], axis=1)
    key_count = prefix_total + cand_length
    block_rows = math.gcd(key_count, 512)
    block_count = key_count // block_rows
    row_total = group_width * cand_length
    row_token = jnp.arange(row_total, dtype=jnp.int32) % cand_length
    starts = jnp.arange(block_count, dtype=jnp.int32) * block_rows

    def attend(carry, block):
        maxima, totals, weighted = carry
        block_keys, block_values, first_row = block
        scores = (
            jnp.einsum("krd,knd->krn", rotated, block_keys, preferred_element_type=jnp.float32)
            * score_scale
        )
        cand_offset = first_row + jnp.arange(block_rows, dtype=jnp.int32) - prefix_total
        scores = jnp.where((cand_offset[None, :] <= row_token[:, None])[None], scores, -jnp.inf)
        highest = jnp.maximum(maxima, jnp.max(scores, axis=-1))
        decline = jnp.exp(maxima - highest)
        exponent = jnp.exp(scores - highest[..., None])
        totals = totals * decline + jnp.sum(exponent, axis=-1)
        weighted = weighted * decline[..., None] + jnp.einsum(
            "krn,knd->krd",
            exponent.astype(jnp.bfloat16),
            block_values,
            preferred_element_type=jnp.float32,
        )
        return ((highest, totals, weighted), None)

    start_state = (
        jnp.full((key_value_rows, row_total), -1e30, jnp.float32),
        jnp.zeros((key_value_rows, row_total), jnp.float32),
        jnp.zeros((key_value_rows, row_total, HEAD_WIDTH), jnp.float32),
    )
    key_blocks = all_keys.reshape(key_value_rows, block_count, block_rows, HEAD_WIDTH).transpose(
        1, 0, 2, 3
    )
    value_blocks = all_values.reshape(
        key_value_rows, block_count, block_rows, HEAD_WIDTH
    ).transpose(1, 0, 2, 3)
    final_state, unused = lax.scan(attend, start_state, (key_blocks, value_blocks, starts))
    maxima, totals, weighted = final_state
    attended = (weighted / totals[..., None]).reshape(head_rows, cand_length, HEAD_WIDTH)
    device_place = lax.axis_index("grp") * sequence_count + lax.axis_index("seq")
    cand_of_row = (device_place * head_rows + jnp.arange(head_rows, dtype=jnp.int32)) // QUERY_HEADS
    cand_slots = jnp.arange(lengths.shape[0], dtype=jnp.int32)
    cand_limit = jnp.sum(
        jnp.where(cand_of_row[:, None] == cand_slots[None, :], lengths[None, :], 0), axis=1
    )
    visible = jnp.arange(cand_length, dtype=jnp.int32)[None, :] < cand_limit[:, None]
    return jnp.where(visible[:, :, None], attended, jnp.float32(0.0)).astype(jnp.bfloat16)


def solution(mesh):
    return jax.shard_map(
        shards,
        mesh=mesh,
        in_specs=(
            P(("grp", "seq"), None, None),
            P(("grp", "seq"), None, None),
            P(("grp", "seq"), None, None),
            P(("grp", "seq"), None),
            P(("grp", "seq"), None),
            P(),
        ),
        out_specs=P(("grp", "seq"), None, None),
        check_vma=False,
    )
```

profile of v0, /device:TPU:0, one launch (start us, length us, event | category | flops | bytes accessed | tf_op | source)
XLA Modules:
  0.0 70.8 jit_solution(9848074302536593648)
XLA Ops:
  0.0 0.7 %pad_clamp_fusion.1 = s32[1024]{0:T(1024)S(1)} fusion(s32[64]{0:T(128)} %constant.134), kind=kLoop, calls=%fused_computation.44 | loop fusion | flops 1024 | bytes 4352 | tf_op jit(solution)/shard_map/jit(_take)/gather | solution.py:44
  0.7 0.7 %pad_maximum_fusion = bf16[4,8,2,128]{3,0,2,1:T(4,128)(2,1)S(1)} fusion(bf16[4,8,1,128]{3,0,2,1:T(4,128)(2,1)} %bitcast.24, bf16[4,8,1,128]{3,0,2,1:T(4,128)(2,1)} %bitcast.25), kind=kLoop, calls=%fused_computation.41 | loop fusion | flops 8192 | bytes 32768 | tf_op jit(solution)/shard_map/stack | solution.py:37
  1.5 0.7 gather_fusion
  2.1 0.1 copy.24
  2.3 0.1 gather.10
  2.3 0.8 %copy.25 = bf16[8,4,2048]{2,1,0:T(4,128)(2,1)} copy(bf16[8,4,2048]{2,0,1:T(8,128)(2,1)S(1)} %bitcast.23) | data formatting | bytes 262144 | tf_op jit(solution)/shard_map/transpose | solution.py:45
  3.1 7.3 %all-to-all-start = ((bf16[8,4,2048]{2,1,0:T(4,128)(2,1)}), bf16[8,4,2048]{2,1,0:T(4,128)(2,1)S(1)}, u32[]{:S(2)}, u32[]{:S(2)}) async-start(bf16[8,4,2048]{2,1,0:T(4,128)(2,1)} %copy.25), calls=%async_computation | async-start | bytes 262144 | tf_op jit(solution)/shard_map/all_to_all | solution.py:71
  10.5 3.2 %convert_element_type.38 = f32[128,128,128]{2,1,0:T(8,128)S(1)} convert(bf16[128,128,128]{2,1,0:T(8,128)(2,1)} %param.10) | non-fusion elementwise | flops 2097152 | bytes 12582912 | tf_op jit(solution)/shard_map/convert_element_type | solution.py:79
  13.7 0.0 copy-done
  13.7 0.1 convert_element_type.40
  13.8 0.3 multiply_cosine_fusion
  14.1 0.0 copy-start.1
  14.2 0.0 copy-start.3
  14.2 5.0 %subtract_convert_fusion = (bf16[128,128,64]{2,1,0:T(8,128)(2,1)}, bf16[128,128,64]{2,1,0:T(8,128)(2,1)}) fusion(f32[128,128,128]{2,1,0:T(8,128)S(1)} %convert_element_type.38, f32[128,64]{1,0:T(8,128)S(1)} %get-tuple-element.39, f32[128,64]{1,0:T(8,128)S(1)} %get-tuple-element.38), kind=kLoop, calls=%fused_computation.15 | loop fusion | flops 8388608 | bytes 12648448 | tf_op jit(solution)/shard_map/convert.5
  19.2 0.4 subtract_convert_fusion.1
  19.6 0.0 copy-done.1
  19.7 0.0 copy-done.3
  19.7 0.1 select_reduce_fusion
  19.8 0.1 iota_compare_fusion
  19.9 0.2 broadcast_compare_fusion
  20.1 0.0 all-to-all-done
  20.1 7.2 %all_gather.3 = bf16[1,128,2048]{2,1,0:T(8,128)(2,1)S(1)} all-gather(bf16[1,32,2048]{2,1,0:T(8,128)(2,1)S(1)} %all_to_all.10), channel_id=1, replica_groups=mesh['grp'=4,'seq'=8] {'grp'}, dimensions={1}, use_global_device_ids=true | all-gather | bytes 655360 | tf_op jit(solution)/shard_map/all_gather | solution.py:72
  27.3 0.4 reshape.191
  27.7 0.7 %fusion.31 = (bf16[128,8,1,128]{3,2,1,0:T(2,128)(2,1)S(1)}, bf16[128,8,1,128]{3,2,1,0:T(2,128)(2,1)S(1)}) fusion(bf16[128,8,2,128]{3,2,1,0:T(2,128)(2,1)S(1)} %reshape.191), kind=kLoop, calls=%fused_computation.61 | loop fusion | bytes 1048576 | tf_op jit(solution)/shard_map/slice | solution.py:76
  28.4 0.2 copy_bitcast_fusion
  28.6 0.6 gather_fusion.1
  29.3 15.3 %fusion = (f32[16,1024]{1,0:T(8,128)S(1)}, f32[16,1024,256]{1,2,0:T(8,128)}) fusion(pred[1024,256]{0,1:T(8,128)(4,1)S(1)} %broadcast_compare_fusion, bf16[16,128,64]{2,1,0:T(8,128)(2,1)S(1)} %get-tuple-element.23, bf16[16,128,64]{2,1,0:T(8,128)(2,1)S(1)} %get-tuple-element.22, bf16[16,128,128]{2,1,0:T(8,128)(2,1)S(1)} %gather_fusion.1, ...), kind=kOutput, calls=%fused_computation.5 | convolution fusion | flops 1097842688 | bytes 22347776 | tf_op jit(solution)/shard_map/while/body/eval_jaxpr/krd,knd->krn/dot_general | solution.py:94
  44.6 0.0 copy-start.2
  44.6 9.3 %fusion.1 = f32[16,1024]{1,0:T(8,128)S(1)} fusion(f32[16,1024,256]{1,2,0:T(8,128)} %get-tuple-element.41, f32[16,1024]{1,0:T(8,128)S(1)} %broadcast_maximum_fusion, pred[1024,256]{0,1:T(8,128)(4,1)S(1)} %broadcast_compare_fusion), kind=kLoop, calls=%fused_computation.6 | loop fusion | flops 16760832 | bytes 17170432 | tf_op jit(solution)/shard_map/while/body/eval_jaxpr/reduce_sum | solution.py:102
  53.9 0.6 gather_fusion.2
  54.5 11.3 %add_divide_fusion = bf16[16,1024,128]{2,1,0:T(8,128)(2,1)S(1)} fusion(f32[16,1024]{1,0:T(8,128)S(1)} %get-tuple-element.37, f32[16,1024]{1,0:T(8,128)S(1)} %get-tuple-element.36, f32[16,1024,256]{1,2,0:T(8,128)} %get-tuple-element.41, f32[16,1024]{1,0:T(8,128)S(1)} %broadcast_maximum_fusion, pred[1024,256]{0,1:T(8,128)(4,1)S(1)} %broadcast_compare_fusion, ...), kind=kOutput, calls=%fused_computation.10 | convolution fusion | flops 1098907648 | bytes 22478848 | tf_op jit(solution)/shard_map/while/body/eval_jaxpr/krn,knd->krd/dot_general | solution.py:103
  65.9 4.9 %select_convert_fusion = bf16[128,128,128]{2,1,0:T(8,128)(2,1)} fusion(bf16[128,128,128]{2,1,0:T(8,128)(2,1)S(1)} %bitcast.21, pred[128,128]{1,0:T(8,128)(4,1)S(1)} %iota_compare_fusion), kind=kLoop, calls=%fused_computation.9 | loop fusion | flops 2097152 | bytes 8404992 | tf_op jit(solution)/shard_map/convert_element_type | solution.py:132
  (11 shorter events, 0.1 us)
Async XLA Ops:
  0.0 13.7 %copy-start = (bf16[16,128,128]{2,1,0:T(8,128)(2,1)S(1)}, bf16[16,128,128]{2,1,0:T(8,128)(2,1)}, u32[]{:S(2)}) copy-start(bf16[16,128,128]{2,1,0:T(8,128)(2,1)} %param.11) | copy-start | bytes 1572868
  3.1 17.0 %all-to-all-start = ((bf16[8,4,2048]{2,1,0:T(4,128)(2,1)}), bf16[8,4,2048]{2,1,0:T(4,128)(2,1)S(1)}, u32[]{:S(2)}, u32[]{:S(2)}) async-start(bf16[8,4,2048]{2,1,0:T(4,128)(2,1)} %copy.25), calls=%async_computation | async-start | bytes 262144 | tf_op jit(solution)/shard_map/all_to_all | solution.py:71
  14.1 5.5 %copy-start.1 = (s32[16]{0:T(128)S(1)}, s32[16]{0:T(128)}, u32[]{:S(2)}) copy-start(s32[16]{0:T(128)} %constant.137) | copy-start | bytes 196
  14.2 5.5 %copy-start.3 = (s32[64]{0:T(128)S(1)}, s32[64]{0:T(128)}, u32[]{:S(2)}) copy-start(s32[64]{0:T(128)} %param.15) | copy-start | bytes 772
  44.6 10.0 %copy-start.2 = (bf16[16,128,128]{2,1,0:T(8,128)(2,1)S(1)}, bf16[16,128,128]{2,1,0:T(8,128)(2,1)}, u32[]{:S(2)}) copy-start(bf16[16,128,128]{2,1,0:T(8,128)(2,1)} %param.12) | copy-start | bytes 1572868
where the time goes:
time: 71.2 us; the launch traced here: 70.8 us
  matrix products  26.6 us (37%)
  other arithmetic  25.2 us (35%)
  starting transfers between devices  7.31 us (10%)
  blocking collectives  7.17 us (10%)
  local copies, waits for them, and re-layouts  4.28 us (6%)
    dot_general x1, matrix products, attend(): jnp.einsum('krd,knd->krn', rotated, block_keys, preferred_element_type=jn...  15.3 us
    dot_general x1, matrix products, attend(): jnp.einsum('krn,knd->krd', exponent.astype(jnp.bfloat16), block_values, p...  11.3 us
    reduce_sum x1, other arithmetic, attend(): totals = totals * decline + jnp.sum(exponent, axis=-1)  9.26 us
    all_to_all x1, starting transfers between devices, shards(): lax.all_to_all(outgoing, 'seq', split_axis=0, concat_axis=1, tiled=True)  7.31 us
    all_gather x1, blocking collectives, shards(): prefix_pair = lax.all_gather(spread, 'grp', axis=1, tiled=True)  7.17 us
    another operation x2, other arithmetic  5.46 us
    convert_element_type x1, other arithmetic, shards(): jnp.where(visible[:, :, None], attended, jnp.float32(0.0))  4.9 us
    convert_element_type x1, other arithmetic, shards(): cand_queries.astype(jnp.float32)  3.25 us
  transfers between devices with their start and end apart: 1, of which 0 were waited for; matrix products, arithmetic and copies ran while one was open for 13% of the time, Pallas kernels for 0%

commit v1 on v0

v1 whole, which is shorter than its diff:
```python
import functools
import math

import jax
import jax.numpy as jnp
import numpy as np
from jax import lax
from jax.experimental import pallas as pl
from jax.experimental.pallas import tpu as pltpu
from jax.sharding import PartitionSpec as P

QUERY_HEADS = 64
KEY_VALUE_HEADS = 8
HEAD_WIDTH = 128

rope_base = 500000.0
exp2_scale = math.log2(math.e) / math.sqrt(HEAD_WIDTH)


def rotation_tables(first, count):
    half_width = HEAD_WIDTH // 2
    exponents = jnp.arange(half_width, dtype=jnp.float32) * (2.0 / HEAD_WIDTH)
    frequency = 1.0 / jnp.power(jnp.float32(rope_base), exponents)
    positions = (first + jnp.arange(count, dtype=jnp.int32)).astype(jnp.float32)
    angles = positions[:, None] * frequency[None, :]
    cosine = jnp.cos(angles)
    sine = jnp.sin(angles)
    return jnp.concatenate([cosine, cosine], axis=1), jnp.concatenate([-sine, sine], axis=1)


def attend_kernel(
    first_row,
    live,
    queries,
    keys,
    values,
    prefix,
    cosine,
    sine,
    out,
    staged,
    sems,
    *,
    heads,
    tile,
):
    rows, tokens, width = keys.shape
    group = queries.shape[0] // rows
    prefix_rows = prefix.shape[0]
    value_base = heads * width
    column = lax.broadcasted_iota(jnp.int32, (tile, tokens), 1)
    token = lax.broadcasted_iota(jnp.int32, (tile, tokens), 0)
    out_token = lax.broadcasted_iota(jnp.int32, (tile, width), 0)

    def rotate(x, start):
        x = x.astype(jnp.float32)
        size = x.shape[-2]
        cos = cosine[start : start + size]
        sin = sine[start : start + size]
        return (x * cos + pltpu.roll(x, width // 2, x.ndim - 1) * sin).astype(jnp.bfloat16)

    def one_row(r, carry):
        head = lax.rem(r, heads)
        length = live[lax.div(first_row[0] + r, KEY_VALUE_HEADS)]
        key_column = pl.multiple_of(head * width, width)
        value_column = pl.multiple_of(value_base + head * width, width)
        all_keys = jnp.concatenate(
            [prefix[:, pl.ds(key_column, width)], rotate(keys[r], 0)], axis=0
        )
        all_values = jnp.concatenate([prefix[:, pl.ds(value_column, width)], values[r]], axis=0)
        all_values = jnp.concatenate([all_values, jnp.ones_like(all_values)], axis=1)
        slot = pl.ds(pl.multiple_of(r * group, group), group)
        for start in range(0, tokens, tile):
            piece = slice(start, start + tile)
            q = rotate(queries[slot, piece, :], start).reshape(group * tile, width)
            scores = lax.dot_general(
                q, all_keys, (((1,), (1,)), ((), ())), preferred_element_type=jnp.float32
            )
            allowed = (column <= token + start)[None]
            own = jnp.where(
                allowed, scores[:, prefix_rows:].reshape(group, tile, tokens), -jnp.inf
            ).reshape(group * tile, tokens)
            scores = jnp.concatenate([scores[:, :prefix_rows], own], axis=1)
            highest = jnp.max(scores, axis=-1, keepdims=True)
            weights = jnp.exp2((scores - highest) * exp2_scale).astype(jnp.bfloat16)
            summed = jnp.dot(weights, all_values, preferred_element_type=jnp.float32)
            attended = summed[:, :width] / summed[:, width:]
            visible = (out_token + start < length)[None]
            attended = jnp.where(visible, attended.reshape(group, tile, width), 0.0)
            staged[slot, piece, :] = attended.astype(jnp.bfloat16)
        pltpu.make_async_copy(staged.at[slot], out.at[slot], sems.at[r]).start()
        return carry

    lax.fori_loop(0, rows, one_row, 0)

    def finish(r, carry):
        slot = pl.ds(pl.multiple_of(r * group, group), group)
        pltpu.make_async_copy(staged.at[slot], out.at[slot], sems.at[r]).wait()
        return carry

    lax.fori_loop(0, rows, finish, 0)


def attend(first_row, lengths, queries, keys, values, prefix, cosine, sine, heads):
    rows = keys.shape[0]
    in_vmem = pl.BlockSpec(memory_space=pltpu.VMEM)
    in_smem = pl.BlockSpec(memory_space=pltpu.SMEM)
    return pl.pallas_call(
        functools.partial(attend_kernel, heads=heads, tile=min(64, keys.shape[1])),
        out_shape=jax.ShapeDtypeStruct(queries.shape, jnp.bfloat16),
        in_specs=[in_smem, in_smem] + [in_vmem] * 6,
        out_specs=pl.BlockSpec(memory_space=pl.ANY),
        scratch_shapes=[
            pltpu.VMEM(queries.shape, jnp.bfloat16),
            pltpu.SemaphoreType.DMA((rows,)),
        ],
        compiler_params=pltpu.CompilerParams(vmem_limit_bytes=40 << 20),
        name="attend",
    )(first_row, lengths, queries, keys, values, prefix, cosine, sine)


def shards(
    cand_queries,
    candidate_keys,
    candidate_values,
    prefix_rotated_keys,
    prefix_value_matrix,
    lengths,
):
    sequence_count = lax.axis_size("seq")
    grp_count = lax.axis_size("grp")
    key_value_rows, cand_length, _ = candidate_keys.shape
    heads = min(KEY_VALUE_HEADS, key_value_rows)
    prefix_here = prefix_rotated_keys.shape[0]
    prefix_total = prefix_here * sequence_count * grp_count
    wanted = (
        np.arange(sequence_count)[:, None] * key_value_rows + np.arange(heads)[None, :]
    ) % KEY_VALUE_HEADS

    def by_target(matrix):
        if (wanted == np.arange(KEY_VALUE_HEADS)[None, :]).all():
            return jnp.broadcast_to(matrix[None], (sequence_count,) + matrix.shape)
        split = matrix.reshape(prefix_here, KEY_VALUE_HEADS, HEAD_WIDTH)
        picked = jnp.take(split, wanted.reshape(-1), axis=1)
        return picked.reshape(prefix_here, sequence_count, heads * HEAD_WIDTH).transpose(1, 0, 2)

    outgoing = jnp.concatenate([by_target(prefix_rotated_keys), by_target(prefix_value_matrix)], axis=2)
    spread = lax.all_to_all(outgoing, "seq", split_axis=0, concat_axis=0, tiled=True)
    spread = spread.reshape(sequence_count * prefix_here, 2 * heads * HEAD_WIDTH)
    prefix = lax.all_gather(spread, "grp", axis=0, tiled=True)
    cosine, sine = rotation_tables(prefix_total, cand_length)
    place = lax.axis_index("grp") * sequence_count + lax.axis_index("seq")
    first_row = (place * key_value_rows).astype(jnp.int32).reshape(1)
    return attend(
        first_row,
        lengths,
        cand_queries,
        candidate_keys,
        candidate_values,
        prefix,
        cosine,
        sine,
        heads,
    )


def solution(mesh):
    return jax.shard_map(
        shards,
        mesh=mesh,
        in_specs=(
            P(("grp", "seq"), None, None),
            P(("grp", "seq"), None, None),
            P(("grp", "seq"), None, None),
            P(("grp", "seq"), None),
            P(("grp", "seq"), None),
            P(),
        ),
        out_specs=P(("grp", "seq"), None, None),
        check_vma=False,
    )
```

time: 71.2 us -> 45.1 us (0.63)
  matrix products: 26.6 us -> 0 us
  other arithmetic: 25.2 us -> 1.15 us
  Pallas kernels: 0 us -> 15.7 us
  waiting for transfers between devices: 0.01 us -> 6.89 us
  local copies, waits for them, and re-layouts: 4.28 us -> 6.39 us
    dot_general x2 -> x0, matrix products: 26.6 us -> none  [the longest x1 15.3 us: attend(): jnp.einsum('krd,knd->krn', rotated, block_keys, preferred_element_type=jn...]
    pallas_call x0 -> x1, Pallas kernels: none -> 15.7 us  [attend(): pl.pallas_call(functools.partial(attend_kernel, heads=heads, tile=min(64,...]
    reduce_sum x2 -> x0, other arithmetic: 9.36 us -> none  [the longest x1 9.26 us: attend(): totals = totals * decline + jnp.sum(exponent, axis=-1)]
    convert_element_type x4 -> x1, other arithmetic: 8.25 us -> 0.01 us  [rotation_tables(): positions = (first + jnp.arange(count, dtype=jnp.int32)).astype(jnp.float32)]
    all_to_all x1, waiting for transfers between devices: 0.01 us -> 6.89 us  [shards(): lax.all_to_all(outgoing, 'seq', split_axis=0, concat_axis=0, tiled=True)]
    another operation x3 -> x0, other arithmetic: 6.19 us -> none
    unnamed x8, local copies, waits for them, and re-layouts: 0.02 us -> 4.92 us
    gather x5 -> x0, local copies, waits for them, and re-layouts: 2.17 us -> none  [the longest x3 0.87 us: pick_heads(): picked = jnp.take(stacked, head_table, axis=1)]
  transfers between devices with their start and end apart: 1 -> 1, of which waited for: 0 -> 1; matrix products, arithmetic and copies ran while one was open for 13% -> 1% of each run, Pallas kernels for 0% -> 0%
where the time goes in v1:
time: 45.1 us; the launch traced here: 44.7 us
  Pallas kernels  15.7 us (35%)
  starting transfers between devices  7.31 us (16%)
  blocking collectives  7.17 us (16%)
  waiting for transfers between devices  6.89 us (15%)
  local copies, waits for them, and re-layouts  6.39 us (14%)
  other arithmetic  1.15 us (3%)
    pallas_call x1, Pallas kernels, attend(): pl.pallas_call(functools.partial(attend_kernel, heads=heads, tile=min(64,...  15.7 us
    all_to_all x1, starting transfers between devices, shards(): lax.all_to_all(outgoing, 'seq', split_axis=0, concat_axis=0, tiled=True)  7.31 us
    all_gather x1, blocking collectives, shards(): prefix = lax.all_gather(spread, 'grp', axis=0, tiled=True)  7.17 us
    all_to_all x1, waiting for transfers between devices, shards(): lax.all_to_all(outgoing, 'seq', split_axis=0, concat_axis=0, tiled=True)  6.89 us
    unnamed x8, local copies, waits for them, and re-layouts  4.92 us
    broadcast_in_dim x2, local copies, waits for them, and re-layouts, by_target(): return jnp.broadcast_to(matrix[None], (sequence_count,) + matrix.shape)  1.44 us
  transfers between devices with their start and end apart: 1, of which 1 were waited for; matrix products, arithmetic and copies ran while one was open for 1% of the time, Pallas kernels for 0%

profile of v1, /device:TPU:0, one launch (start us, length us, event | category | flops | bytes accessed | tf_op | source)
XLA Modules:
  0.0 44.7 jit_solution(1942063199727499350)
XLA Ops:
  0.0 0.7 %broadcast_in_dim.4 = bf16[8,4,1024]{2,1,0:T(4,128)(2,1)S(1)} broadcast(bf16[4,1024]{1,0:T(4,128)(2,1)} %param.9), dimensions={1,2} | broadcast | bytes 73728 | tf_op jit(solution)/shard_map/broadcast_in_dim | solution.py:142
  0.7 0.7 %broadcast_in_dim.5 = bf16[8,4,1024]{2,1,0:T(4,128)(2,1)S(1)} broadcast(bf16[4,1024]{1,0:T(4,128)(2,1)} %param.10), dimensions={1,2} | broadcast | bytes 73728 | tf_op jit(solution)/shard_map/broadcast_in_dim | solution.py:142
  1.4 0.7 %pad_maximum_fusion = bf16[8,4,2048]{2,1,0:T(4,128)(2,1)} fusion(bf16[8,4,1024]{2,1,0:T(4,128)(2,1)S(1)} %broadcast_in_dim.5, bf16[8,4,1024]{2,1,0:T(4,128)(2,1)S(1)} %broadcast_in_dim.4), kind=kLoop, calls=%fused_computation | loop fusion | flops 262144 | bytes 262144 | tf_op jit(solution)/shard_map/concatenate | solution.py:147
  2.2 7.3 %all-to-all-start = ((bf16[8,4,2048]{2,1,0:T(4,128)(2,1)}), bf16[8,4,2048]{2,1,0:T(4,128)(2,1)S(1)}, u32[]{:S(2)}, u32[]{:S(2)}) async-start(bf16[8,4,2048]{2,1,0:T(4,128)(2,1)} %pad_maximum_fusion), calls=%async_computation | async-start | bytes 262144 | tf_op jit(solution)/shard_map/all_to_all | solution.py:148
  9.5 0.3 fusion
  9.8 0.1 pad_maximum_fusion.1
  9.9 6.9 %all-to-all-done = bf16[8,4,2048]{2,1,0:T(4,128)(2,1)S(1)} async-done(((bf16[8,4,2048]{2,1,0:T(4,128)(2,1)}), bf16[8,4,2048]{2,1,0:T(4,128)(2,1)S(1)}, u32[]{:S(2)}, u32[]{:S(2)}) %all-to-all-start) | async-done | bytes 131104 | tf_op jit(solution)/shard_map/all_to_all | solution.py:148
  16.9 7.2 %all_gather.3.prefix = bf16[128,2048]{1,0:T(8,128)(2,1)S(1)} all-gather(bf16[32,2048]{1,0:T(8,128)(2,1)S(1)} %reshape.20), channel_id=1, replica_groups=mesh['grp'=4,'seq'=8] {'grp'}, dimensions={0}, use_global_device_ids=true | all-gather | bytes 655360 | tf_op jit(solution)/shard_map/all_gather | solution.py:150
  24.0 0.0 copy-start
  24.0 2.2 %copy-done = bf16[128,128,128]{2,1,0:T(8,128)(2,1)S(1)} copy-done((bf16[128,128,128]{2,1,0:T(8,128)(2,1)S(1)}, bf16[128,128,128]{2,1,0:T(8,128)(2,1)}, u32[]{:S(2)}) %copy-start) | copy-done | bytes 4194328
  26.2 0.0 copy-start.1
  26.2 1.0 %copy-done.1 = bf16[16,128,128]{2,1,0:T(8,128)(2,1)S(1)} copy-done((bf16[16,128,128]{2,1,0:T(8,128)(2,1)S(1)}, bf16[16,128,128]{2,1,0:T(8,128)(2,1)}, u32[]{:S(2)}) %copy-start.1) | copy-done | bytes 524312
  27.3 0.0 copy-start.2
  27.3 1.0 %copy-done.2 = bf16[16,128,128]{2,1,0:T(8,128)(2,1)S(1)} copy-done((bf16[16,128,128]{2,1,0:T(8,128)(2,1)S(1)}, bf16[16,128,128]{2,1,0:T(8,128)(2,1)}, u32[]{:S(2)}) %copy-start.2) | copy-done | bytes 524312
  28.3 0.0 copy-start.3
  28.3 0.7 %copy-done.3 = s32[64]{0:T(128)S(1)} copy-done((s32[64]{0:T(128)S(1)}, s32[64]{0:T(128)}, u32[]{:S(2)}) %copy-start.3) | copy-done | bytes 280
  29.0 15.7 %attend.1 = bf16[128,128,128]{2,1,0:T(8,128)(2,1)} custom-call(s32[1]{0:T(128)} %bitcast.first_row, s32[64]{0:T(128)S(1)} %copy-done.3, bf16[128,128,128]{2,1,0:T(8,128)(2,1)S(1)} %copy-done, bf16[16,128,128]{2,1,0:T(8,128)(2,1)S(1)} %copy-done.1, bf16[16,128,128]{2,1,0:T(8,128)(2,1)S(1)} %copy-done.2, bf16[128,2048]{1,0:T(8,128)(2,1)S(1)} %all_gather.3.prefix, ...), custom_call_target="tpu_custom_call" | custom-call | tf_op jit(solution)/shard_map/attend/pallas_call | solution.py:108
  (3 shorter events, 0.0 us)
Async XLA Ops:
  2.2 14.7 %all-to-all-start = ((bf16[8,4,2048]{2,1,0:T(4,128)(2,1)}), bf16[8,4,2048]{2,1,0:T(4,128)(2,1)S(1)}, u32[]{:S(2)}, u32[]{:S(2)}) async-start(bf16[8,4,2048]{2,1,0:T(4,128)(2,1)} %pad_maximum_fusion), calls=%async_computation | async-start | bytes 262144 | tf_op jit(solution)/shard_map/all_to_all | solution.py:148
  24.0 2.2 %copy-start = (bf16[128,128,128]{2,1,0:T(8,128)(2,1)S(1)}, bf16[128,128,128]{2,1,0:T(8,128)(2,1)}, u32[]{:S(2)}) copy-start(bf16[128,128,128]{2,1,0:T(8,128)(2,1)} %queries.1) | copy-start | bytes 12582916
  26.2 1.0 %copy-start.1 = (bf16[16,128,128]{2,1,0:T(8,128)(2,1)S(1)}, bf16[16,128,128]{2,1,0:T(8,128)(2,1)}, u32[]{:S(2)}) copy-start(bf16[16,128,128]{2,1,0:T(8,128)(2,1)} %keys.1) | copy-start | bytes 1572868
  27.3 1.0 %copy-start.2 = (bf16[16,128,128]{2,1,0:T(8,128)(2,1)S(1)}, bf16[16,128,128]{2,1,0:T(8,128)(2,1)}, u32[]{:S(2)}) copy-start(bf16[16,128,128]{2,1,0:T(8,128)(2,1)} %values.1) | copy-start | bytes 1572868
  28.3 0.7 %copy-start.3 = (s32[64]{0:T(128)S(1)}, s32[64]{0:T(128)}, u32[]{:S(2)}) copy-start(s32[64]{0:T(128)} %live.1) | copy-start | bytes 772

commit v2 on v1

v2 whole, which is shorter than its diff:
```python
import functools
import math

import jax
import jax.numpy as jnp
import numpy as np
from jax import lax
from jax.experimental import pallas as pl
from jax.experimental.pallas import tpu as pltpu
from jax.sharding import PartitionSpec as P

QUERY_HEADS = 64
KEY_VALUE_HEADS = 8
HEAD_WIDTH = 128

rope_base = 500000.0
exp2_scale = math.log2(math.e) / math.sqrt(HEAD_WIDTH)
score_chunk = 64
rotate_vmem = 51_000_000


def rotation_tables(first, count):
    half_width = HEAD_WIDTH // 2
    exponents = jnp.arange(half_width, dtype=jnp.float32) * (2.0 / HEAD_WIDTH)
    frequency = 1.0 / jnp.power(jnp.float32(rope_base), exponents)
    positions = (first + jnp.arange(count, dtype=jnp.int32)).astype(jnp.float32)
    angles = positions[:, None] * frequency[None, :]
    cosine = jnp.cos(angles)
    sine = jnp.sin(angles)
    return jnp.concatenate([cosine, cosine], axis=1), jnp.concatenate([-sine, sine], axis=1)


def rows_of(index, count):
    return pl.ds(pl.multiple_of(index * count, count), count)


def rotate_kernel(cosine, sine, queries, keys, out_q, out_k, raw_q, raw_k, q_sems, key_sem):
    rows, tokens, width = keys.shape
    group = queries.shape[0] // rows

    def load(r):
        span = rows_of(r, group)
        return pltpu.make_async_copy(queries.at[span], raw_q.at[span], q_sems.at[r])

    keys_in = pltpu.make_async_copy(keys, raw_k, key_sem)

    def start(r, carry):
        load(r).start()
        return carry

    lax.fori_loop(0, rows, start, 0)
    keys_in.start()

    def rotate(x):
        x = x.astype(jnp.float32)
        turned = pltpu.roll(x, width // 2, x.ndim - 1)
        return (x * cosine[...] + turned * sine[...]).astype(jnp.bfloat16)

    def one_row(r, carry):
        load(r).wait()
        span = rows_of(r, group)
        out_q[span] = rotate(raw_q[span])
        return carry

    lax.fori_loop(0, rows, one_row, 0)
    keys_in.wait()

    def one_key_row(r, carry):
        out_k[r] = rotate(raw_k[r])
        return carry

    lax.fori_loop(0, rows, one_key_row, 0)


def rotated(cosine, sine, queries, keys):
    rows = keys.shape[0]
    in_vmem = pl.BlockSpec(memory_space=pltpu.VMEM)
    in_hbm = pl.BlockSpec(memory_space=pltpu.HBM)
    shape = lambda x: jax.ShapeDtypeStruct(x.shape, jnp.bfloat16)
    return pl.pallas_call(
        rotate_kernel,
        out_shape=[shape(queries), shape(keys)],
        in_specs=[in_vmem] * 2 + [in_hbm] * 2,
        out_specs=[in_vmem] * 2,
        scratch_shapes=[
            pltpu.VMEM(queries.shape, jnp.bfloat16),
            pltpu.VMEM(keys.shape, jnp.bfloat16),
            pltpu.SemaphoreType.DMA((rows,)),
            pltpu.SemaphoreType.DMA(()),
        ],
        cost_estimate=pl.CostEstimate(
            flops=6 * queries.size, bytes_accessed=2 * queries.size, transcendentals=0
        ),
        compiler_params=pltpu.CompilerParams(vmem_limit_bytes=rotate_vmem),
        name="rotate",
    )(cosine, sine, queries, keys)


def attend_kernel(live, queries, keys, values, prefix, out, staged, *scratch, heads, block, tile):
    score_slots, weight_slots, sems = scratch[:2], scratch[2:4], scratch[4]
    rows, tokens, width = keys.shape
    group = queries.shape[0] // rows
    prefix_rows = prefix.shape[0]
    value_base = heads * width
    place = lax.axis_index("grp") * lax.axis_size("seq") + lax.axis_index("seq")
    column = lax.broadcasted_iota(jnp.int32, (tile, tokens), 1)
    token = lax.broadcasted_iota(jnp.int32, (tile, tokens), 0)
    out_token = lax.broadcasted_iota(jnp.int32, (tokens, width), 0)

    def score(r, count, slot):
        column_start = pl.multiple_of(lax.rem(r, heads) * width, width)
        all_keys = jnp.concatenate([prefix[:, pl.ds(column_start, width)], keys[r]], axis=0)
        q = queries[rows_of(r, group), :count, :].reshape(group * count, width)
        score_slots[slot][: group * count] = lax.dot_general(
            q, all_keys, (((1,), (1,)), ((), ())), preferred_element_type=jnp.float32
        )

    def weigh(count, slot):
        for start in range(0, group * count, tile):
            s = score_slots[slot][start : start + tile]
            own = jnp.where(column <= token + start % count, s[:, prefix_rows:], -jnp.inf)
            s = jnp.concatenate([s[:, :prefix_rows], own], axis=1)
            highest = jnp.max(s, axis=-1, keepdims=True)
            weights = jnp.exp2((s - highest) * exp2_scale)
            weight_slots[slot][start : start + tile] = weights.astype(jnp.bfloat16)

    def gather_values(r, count, length, slot):
        column_start = pl.multiple_of(value_base + lax.rem(r, heads) * width, width)
        all_values = jnp.concatenate([prefix[:, pl.ds(column_start, width)], values[r]], axis=0)
        all_values = jnp.concatenate([all_values, jnp.ones_like(all_values)], axis=1)
        summed = jnp.dot(
            weight_slots[slot][: group * count], all_values, preferred_element_type=jnp.float32
        )
        attended = (summed[:, :width] / summed[:, width:]).astype(jnp.bfloat16)
        attended = attended.reshape(group, count, width)
        span = rows_of(r, group)
        visible = (out_token[:count] < length)[None]
        staged[span, :count, :] = jnp.where(visible, attended, jnp.zeros_like(attended))
        if count < tokens:
            staged[span, count:, :] = jnp.zeros((group, tokens - count, width), jnp.bfloat16)
        pltpu.make_async_copy(staged.at[span], out.at[span], sems.at[r]).start()

    def block_of_rows(base, count, length):
        score(base, count, 0)
        for u in range(block):
            slot = u % 2
            if u + 1 < block:
                score(base + u + 1, count, 1 - slot)
            weigh(count, slot)
            gather_values(base + u, count, length, slot)

    def one_block(index, carry):
        base = index * block
        length = live[lax.div(place * rows + base, KEY_VALUE_HEADS)]
        tiles = jnp.clip(lax.div(length + tile - 1, tile), 1, tokens // tile)
        for n in range(1, tokens // tile + 1):
            pl.when(tiles == n)(functools.partial(block_of_rows, base, n * tile, length))
        return carry

    lax.fori_loop(0, rows // block, one_block, 0)

    def finish(r, carry):
        span = rows_of(r, group)
        pltpu.make_async_copy(staged.at[span], out.at[span], sems.at[r]).wait()
        return carry

    lax.fori_loop(0, rows, finish, 0)


def attend(lengths, queries, keys, values, prefix, heads):
    rows, tokens, _ = keys.shape
    group = queries.shape[0] // rows
    in_vmem = pl.BlockSpec(memory_space=pltpu.VMEM)
    in_smem = pl.BlockSpec(memory_space=pltpu.SMEM)
    wide = (group * tokens, prefix.shape[0] + tokens)
    return pl.pallas_call(
        functools.partial(
            attend_kernel,
            heads=heads,
            block=math.gcd(rows, KEY_VALUE_HEADS),
            tile=math.gcd(tokens, 32),
        ),
        out_shape=jax.ShapeDtypeStruct(queries.shape, jnp.bfloat16),
        in_specs=[in_smem] + [in_vmem] * 4,
        out_specs=pl.BlockSpec(memory_space=pl.ANY),
        scratch_shapes=[pltpu.VMEM(queries.shape, jnp.bfloat16)]
        + [pltpu.VMEM(wide, jnp.float32)] * 2
        + [pltpu.VMEM(wide, jnp.bfloat16)] * 2
        + [pltpu.SemaphoreType.DMA((rows,))],
        compiler_params=pltpu.CompilerParams(vmem_limit_bytes=36 << 20),
        name="attend",
    )(lengths, queries, keys, values, prefix)


def shards(
    cand_queries,
    candidate_keys,
    candidate_values,
    prefix_rotated_keys,
    prefix_value_matrix,
    lengths,
):
    sequence_count = lax.axis_size("seq")
    grp_count = lax.axis_size("grp")
    key_value_rows, cand_length, _ = candidate_keys.shape
    heads = min(KEY_VALUE_HEADS, key_value_rows)
    prefix_total = prefix_rotated_keys.shape[0] * sequence_count * grp_count
    wanted = (
        np.arange(sequence_count)[:, None] * key_value_rows + np.arange(heads)[None, :]
    ) % KEY_VALUE_HEADS

    def by_target(matrix):
        split = matrix.reshape(matrix.shape[0], KEY_VALUE_HEADS, HEAD_WIDTH)
        picked = jnp.take(split, wanted.reshape(-1), axis=1)
        return picked.reshape(matrix.shape[0], sequence_count, heads * HEAD_WIDTH).transpose(1, 0, 2)

    near_seq = math.gcd(sequence_count, 2)
    near_grp = math.gcd(grp_count, 2)
    far_seq, far_grp = sequence_count // near_seq, grp_count // near_grp

    def moved(block, far_g, near_g, far_s, near_s):
        if not (far_g or near_g or far_s or near_s):
            return block
        pairs = []
        for source in range(grp_count * sequence_count):
            g, s = divmod(source, sequence_count)
            g = (g // near_grp + far_g) % far_grp * near_grp + (g + near_g) % near_grp
            s = (s // near_seq + far_s) % far_seq * near_seq + (s + near_s) % near_seq
            pairs.append((source, g * sequence_count + s))
        return lax.ppermute(block, ("grp", "seq"), pairs)

    cosine, sine = rotation_tables(prefix_total, cand_length)
    queries, keys = rotated(cosine, sine, cand_queries, candidate_keys)
    if key_value_rows % KEY_VALUE_HEADS == 0:
        spare = prefix_rotated_keys.shape[1]
        zero = jnp.zeros((), jnp.bfloat16)
        block = lax.pad(prefix_rotated_keys, zero, ((0, 0, 0), (0, spare, 0))) + lax.pad(
            prefix_value_matrix, zero, ((0, 0, 0), (spare, 0, 0))
        )
        block = jnp.concatenate([moved(block, 0, 0, d, 0) for d in range(far_seq)], axis=0)
        block, queries, keys = lax.optimization_barrier((block, queries, keys))
        block = jnp.concatenate(
            [moved(block, e, 0, 0, d) for e in range(far_grp) for d in range(near_seq)], axis=0
        )
        prefix = jnp.concatenate([moved(block, 0, e, 0, 0) for e in range(near_grp)], axis=0)
    else:
        outgoing = jnp.concatenate(
            [by_target(prefix_rotated_keys), by_target(prefix_value_matrix)], axis=2
        )
        spread = lax.all_to_all(outgoing, "seq", split_axis=0, concat_axis=0, tiled=True)
        spread = spread.reshape(-1, 2 * heads * HEAD_WIDTH)
        prefix = lax.all_gather(spread, "grp", axis=0, tiled=True)
    values = candidate_values
    return attend(lengths, queries, keys, values, prefix, heads)


def solution(mesh):
    return jax.shard_map(
        shards,
        mesh=mesh,
        in_specs=(
            P(("grp", "seq"), None, None),
            P(("grp", "seq"), None, None),
            P(("grp", "seq"), None, None),
            P(("grp", "seq"), None),
            P(("grp", "seq"), None),
            P(),
        ),
        out_specs=P(("grp", "seq"), None, None),
        check_vma=False,
    )
```

time: 45.1 us -> 28.8 us (0.64)
  the two profiles are of different devices: /device:TPU:0 before, /device:TPU:1 now
where the time goes in v2:
time: 28.8 us; the launch traced here: 28.4 us
  Pallas kernels  11.3 us (39%)
  starting transfers between devices  9.9 us (34%)
  waiting for transfers between devices  4.77 us (17%)
  other arithmetic  1.27 us (4%)
  local copies, waits for them, and re-layouts  1.08 us (4%)
    ppermute x7, starting transfers between devices, moved(): return lax.ppermute(block, ('grp', 'seq'), pairs)  9.9 us
    pallas_call x1, Pallas kernels, attend(): pl.pallas_call(functools.partial(attend_kernel, heads=heads, block=math.g...  6.5 us
    ppermute x7, waiting for transfers between devices, moved(): return lax.ppermute(block, ('grp', 'seq'), pairs)  4.77 us
    pallas_call x1, Pallas kernels, rotated(): pl.pallas_call(rotate_kernel, out_shape=[shape(queries), shape(keys)], in...  4.76 us
    unnamed x10, local copies, waits for them, and re-layouts  1.07 us
    add x1, other arithmetic, shards(): lax.pad(prefix_rotated_keys, zero, ((0, 0, 0), (0, spare, 0)))  0.78 us
  transfers between devices with their start and end apart: 7, of which 4 were waited for; matrix products, arithmetic and copies ran while one was open for 2% of the time, Pallas kernels for 17%

profile of v2, /device:TPU:1, one launch (start us, length us, event | category | flops | bytes accessed | tf_op | source)
XLA Modules:
  0.0 28.4 jit_solution(13058825774324552465)
XLA Ops:
  0.0 0.0 copy-start.2
  0.0 0.0 copy-start.1
  0.0 0.8 %pad_add_fusion = bf16[4,2048]{1,0:T(4,128)(2,1)S(1)} fusion(bf16[4,1024]{1,0:T(4,128)(2,1)} %param.10, bf16[4,1024]{1,0:T(4,128)(2,1)} %param.9), kind=kLoop, calls=%fused_computation.7 | loop fusion | flops 32768 | bytes 32768 | tf_op jit(solution)/shard_map/add | solution.py:237
  0.8 4.2 %collective-permute-start.2 = (bf16[4,2048]{1,0:T(4,128)(2,1)S(1)}, bf16[4,2048]{1,0:T(4,128)(2,1)S(1)}, u32[]{:S(2)}, u32[]{:S(2)}) collective-permute-start(bf16[4,2048]{1,0:T(4,128)(2,1)S(1)} %pad_add_fusion), channel_id=1, source_target_pairs={{0,6},{1,7},{2,0},{3,1},{4,2},{5,3},{6,4},{7,5},{8,14},{9,15},{10,... | collective-permute-start | bytes 49160 | tf_op jit(solution)/shard_map/ppermute | solution.py:230
  5.0 0.0 collective-permute-start.1
  5.0 0.5 %collective-permute-start = (bf16[4,2048]{1,0:T(4,128)(2,1)S(1)}, bf16[4,2048]{1,0:T(4,128)(2,1)S(1)}, u32[]{:S(2)}, u32[]{:S(2)}) collective-permute-start(bf16[4,2048]{1,0:T(4,128)(2,1)S(1)} %pad_add_fusion), channel_id=1, source_target_pairs={{0,2},{1,3},{2,4},{3,5},{4,6},{5,7},{6,0},{7,1},{8,10},{9,11},{10,... | collective-permute-start | bytes 49160 | tf_op jit(solution)/shard_map/ppermute | solution.py:230
  5.5 0.3 %fusion = (f32[128,64]{1,0:T(8,128)S(1)}, f32[128,64]{1,0:T(8,128)S(1)}, f32[128,64]{1,0:T(8,128)S(1)}) fusion(f32[64]{0:T(128)S(1)} %negate_power_fusion, f32[128]{0:T(128)S(1)} %add_convert_fusion), kind=kLoop, calls=%fused_computation.6 | loop fusion | flops 16384 | bytes 99072 | tf_op jit(solution)/shard_map/neg | solution.py:30
  5.8 0.1 pad_maximum_fusion.2
  5.9 0.0 copy-start
  5.9 1.0 %copy-done = bf16[16,128,128]{2,1,0:T(8,128)(2,1)S(1)} copy-done((bf16[16,128,128]{2,1,0:T(8,128)(2,1)S(1)}, bf16[16,128,128]{2,1,0:T(8,128)(2,1)}, u32[]{:S(2)}) %copy-start) | copy-done | bytes 524312
  6.9 4.8 %rotate.1 = (bf16[128,128,128]{2,1,0:T(8,128)(2,1)S(1)}, bf16[16,128,128]{2,1,0:T(8,128)(2,1)S(1)}) custom-call(f32[128,128]{1,0:T(8,128)S(1)} %get-tuple-element.18.cosine, f32[128,128]{1,0:T(8,128)S(1)} %get-tuple-element.19.sine, bf16[128,128,128]{2,1,0:T(8,128)(2,1)} %queries.1, bf16[16,128,128]{2,1,0:T(8,128)(2,1)S(1)} %copy-done), custom_call_target="tpu_custom_call" | custom-call | flops 12582912 | bytes 4194304 | tf_op jit(solution)/shard_map/rotate/pallas_call | solution.py:80
  11.7 0.0 collective-permute-done.2
  11.7 0.0 collective-permute-done.1
  11.7 0.0 collective-permute-done
  11.8 2.2 %collective-permute-start.5 = (bf16[16,2048]{1,0:T(8,128)(2,1)S(1)}, bf16[16,2048]{1,0:T(8,128)(2,1)S(1)}, u32[]{:S(2)}, u32[]{:S(2)}) collective-permute-start(bf16[16,2048]{1,0:T(8,128)(2,1)S(1)} %pad_maximum_fusion.1), channel_id=1, source_target_pairs={{0,17},{1,16},{2,19},{3,18},{4,21},{5,20},{6,23},{7,22},{8,25},{9,... | collective-permute-start | bytes 196616 | tf_op jit(solution)/shard_map/ppermute | solution.py:230
  14.0 0.3 collective-permute-start.4
  14.3 0.2 collective-permute-start.3
  14.5 1.4 %collective-permute-done.5 = bf16[16,2048]{1,0:T(8,128)(2,1)S(1)} collective-permute-done((bf16[16,2048]{1,0:T(8,128)(2,1)S(1)}, bf16[16,2048]{1,0:T(8,128)(2,1)S(1)}, u32[]{:S(2)}, u32[]{:S(2)}) %collective-permute-start.5) | collective-permute-done | bytes 65568 | tf_op jit(solution)/shard_map/ppermute | solution.py:230
  15.9 1.3 %collective-permute-done.4 = bf16[16,2048]{1,0:T(8,128)(2,1)S(1)} collective-permute-done((bf16[16,2048]{1,0:T(8,128)(2,1)S(1)}, bf16[16,2048]{1,0:T(8,128)(2,1)S(1)}, u32[]{:S(2)}, u32[]{:S(2)}) %collective-permute-start.4) | collective-permute-done | bytes 65568 | tf_op jit(solution)/shard_map/ppermute | solution.py:230
  17.1 1.0 %collective-permute-done.3 = bf16[16,2048]{1,0:T(8,128)(2,1)S(1)} collective-permute-done((bf16[16,2048]{1,0:T(8,128)(2,1)S(1)}, bf16[16,2048]{1,0:T(8,128)(2,1)S(1)}, u32[]{:S(2)}, u32[]{:S(2)}) %collective-permute-start.3) | collective-permute-done | bytes 65568 | tf_op jit(solution)/shard_map/ppermute | solution.py:230
  18.1 2.5 %collective-permute-start.6 = (bf16[64,2048]{1,0:T(8,128)(2,1)S(1)}, bf16[64,2048]{1,0:T(8,128)(2,1)S(1)}, u32[]{:S(2)}, u32[]{:S(2)}) collective-permute-start(bf16[64,2048]{1,0:T(8,128)(2,1)S(1)} %pad_maximum_fusion), channel_id=1, source_target_pairs={{0,8},{1,9},{2,10},{3,11},{4,12},{5,13},{6,14},{7,15},{8,0},{9,1},... | collective-permute-start | bytes 786440 | tf_op jit(solution)/shard_map/ppermute | solution.py:230
  20.7 1.1 %collective-permute-done.6 = bf16[64,2048]{1,0:T(8,128)(2,1)S(1)} collective-permute-done((bf16[64,2048]{1,0:T(8,128)(2,1)S(1)}, bf16[64,2048]{1,0:T(8,128)(2,1)S(1)}, u32[]{:S(2)}, u32[]{:S(2)}) %collective-permute-start.6) | collective-permute-done | bytes 262176 | tf_op jit(solution)/shard_map/ppermute | solution.py:230
  21.9 0.0 copy-done.2
  21.9 0.0 copy-done.1
  21.9 6.5 %attend.1 = bf16[128,128,128]{2,1,0:T(8,128)(2,1)} custom-call(s32[64]{0:T(128)S(1)} %copy-done.2, bf16[128,128,128]{2,1,0:T(8,128)(2,1)S(1)} %get-tuple-element.12.queries, bf16[16,128,128]{2,1,0:T(8,128)(2,1)S(1)} %get-tuple-element.13.keys, bf16[16,128,128]{2,1,0:T(8,128)(2,1)S(1)} %copy-done.1, bf16[128,2048]{1,0:T(8,128)(2,1)S(1)} %constant_dynamic-update-slice_fusion.prefix), custom_call_target="tpu_custom_call" | custom-call | tf_op jit(solution)/shard_map/attend/pallas_call | solution.py:176
  (9 shorter events, 0.1 us)
Async XLA Ops:
  0.0 21.9 %copy-start.2 = (s32[64]{0:T(128)S(1)}, s32[64]{0:T(128)}, u32[]{:S(2)}) copy-start(s32[64]{0:T(128)} %live.1) | copy-start | bytes 772
  0.0 21.9 %copy-start.1 = (bf16[16,128,128]{2,1,0:T(8,128)(2,1)S(1)}, bf16[16,128,128]{2,1,0:T(8,128)(2,1)}, u32[]{:S(2)}) copy-start(bf16[16,128,128]{2,1,0:T(8,128)(2,1)} %values.1) | copy-start | bytes 1572868
  0.8 10.9 %collective-permute-start.2 = (bf16[4,2048]{1,0:T(4,128)(2,1)S(1)}, bf16[4,2048]{1,0:T(4,128)(2,1)S(1)}, u32[]{:S(2)}, u32[]{:S(2)}) collective-permute-start(bf16[4,2048]{1,0:T(4,128)(2,1)S(1)} %pad_add_fusion), channel_id=1, source_target_pairs={{0,6},{1,7},{2,0},{3,1},{4,2},{5,3},{6,4},{7,5},{8,14},{9,15},{10,... | collective-permute-start | bytes 49160 | tf_op jit(solution)/shard_map/ppermute | solution.py:230
  5.0 6.7 %collective-permute-start.1 = (bf16[4,2048]{1,0:T(4,128)(2,1)S(1)}, bf16[4,2048]{1,0:T(4,128)(2,1)S(1)}, u32[]{:S(2)}, u32[]{:S(2)}) collective-permute-start(bf16[4,2048]{1,0:T(4,128)(2,1)S(1)} %pad_add_fusion), channel_id=1, source_target_pairs={{0,4},{1,5},{2,6},{3,7},{4,0},{5,1},{6,2},{7,3},{8,12},{9,13},{10,... | collective-permute-start | bytes 49160 | tf_op jit(solution)/shard_map/ppermute | solution.py:230
  5.0 6.7 %collective-permute-start = (bf16[4,2048]{1,0:T(4,128)(2,1)S(1)}, bf16[4,2048]{1,0:T(4,128)(2,1)S(1)}, u32[]{:S(2)}, u32[]{:S(2)}) collective-permute-start(bf16[4,2048]{1,0:T(4,128)(2,1)S(1)} %pad_add_fusion), channel_id=1, source_target_pairs={{0,2},{1,3},{2,4},{3,5},{4,6},{5,7},{6,0},{7,1},{8,10},{9,11},{10,... | collective-permute-start | bytes 49160 | tf_op jit(solution)/shard_map/ppermute | solution.py:230
  5.9 1.0 %copy-start = (bf16[16,128,128]{2,1,0:T(8,128)(2,1)S(1)}, bf16[16,128,128]{2,1,0:T(8,128)(2,1)}, u32[]{:S(2)}) copy-start(bf16[16,128,128]{2,1,0:T(8,128)(2,1)} %keys.1) | copy-start | bytes 1572868
  11.8 4.1 %collective-permute-start.5 = (bf16[16,2048]{1,0:T(8,128)(2,1)S(1)}, bf16[16,2048]{1,0:T(8,128)(2,1)S(1)}, u32[]{:S(2)}, u32[]{:S(2)}) collective-permute-start(bf16[16,2048]{1,0:T(8,128)(2,1)S(1)} %pad_maximum_fusion.1), channel_id=1, source_target_pairs={{0,17},{1,16},{2,19},{3,18},{4,21},{5,20},{6,23},{7,22},{8,25},{9,... | collective-permute-start | bytes 196616 | tf_op jit(solution)/shard_map/ppermute | solution.py:230
  14.0 3.1 %collective-permute-start.4 = (bf16[16,2048]{1,0:T(8,128)(2,1)S(1)}, bf16[16,2048]{1,0:T(8,128)(2,1)S(1)}, u32[]{:S(2)}, u32[]{:S(2)}) collective-permute-start(bf16[16,2048]{1,0:T(8,128)(2,1)S(1)} %pad_maximum_fusion.1), channel_id=1, source_target_pairs={{0,16},{1,17},{2,18},{3,19},{4,20},{5,21},{6,22},{7,23},{8,24},{9,... | collective-permute-start | bytes 196616 | tf_op jit(solution)/shard_map/ppermute | solution.py:230
  14.3 3.9 %collective-permute-start.3 = (bf16[16,2048]{1,0:T(8,128)(2,1)S(1)}, bf16[16,2048]{1,0:T(8,128)(2,1)S(1)}, u32[]{:S(2)}, u32[]{:S(2)}) collective-permute-start(bf16[16,2048]{1,0:T(8,128)(2,1)S(1)} %pad_maximum_fusion.1), channel_id=1, source_target_pairs={{0,1},{1,0},{2,3},{3,2},{4,5},{5,4},{6,7},{7,6},{8,9},{9,8},{10,11... | collective-permute-start | bytes 196616 | tf_op jit(solution)/shard_map/ppermute | solution.py:230
  18.1 3.7 %collective-permute-start.6 = (bf16[64,2048]{1,0:T(8,128)(2,1)S(1)}, bf16[64,2048]{1,0:T(8,128)(2,1)S(1)}, u32[]{:S(2)}, u32[]{:S(2)}) collective-permute-start(bf16[64,2048]{1,0:T(8,128)(2,1)S(1)} %pad_maximum_fusion), channel_id=1, source_target_pairs={{0,8},{1,9},{2,10},{3,11},{4,12},{5,13},{6,14},{7,15},{8,0},{9,1},... | collective-permute-start | bytes 786440 | tf_op jit(solution)/shard_map/ppermute | solution.py:230

commit v3 on v2

v3 whole, which is shorter than its diff:
```python
import functools
import math

import jax
import jax.numpy as jnp
import numpy as np
from jax import lax
from jax.experimental import pallas as pl
from jax.experimental.pallas import tpu as pltpu
from jax.sharding import PartitionSpec as P

QUERY_HEADS = 64
KEY_VALUE_HEADS = 8
HEAD_WIDTH = 128

rope_base = 500000.0
exp2_scale = math.log2(math.e) / math.sqrt(HEAD_WIDTH)
overflow_margin = 64.0
prepare_vmem = (47_000_000, 38_000_000)
attend_vmem = 20_000_000


def rotation_tables(first, count):
    half_width = HEAD_WIDTH // 2
    exponents = jnp.arange(half_width, dtype=jnp.float32) * (2.0 / HEAD_WIDTH)
    frequency = 1.0 / jnp.power(jnp.float32(rope_base), exponents)
    positions = (first + jnp.arange(count, dtype=jnp.int32)).astype(jnp.float32)
    angles = positions[:, None] * frequency[None, :]
    cosine = jnp.cos(angles)
    sine = jnp.sin(angles)
    return jnp.concatenate([cosine, cosine], axis=1), jnp.concatenate([-sine, sine], axis=1)


def rows_of(index, count):
    return pl.ds(pl.multiple_of(index * count, count), count)


def prepare_kernel(
    cosine,
    sine,
    queries,
    keys,
    out_q,
    out_k,
    out_w,
    out_m,
    raw_q,
    raw_k,
    scores_a,
    scores_b,
    q_sems,
    key_sem,
    *,
    first,
    tile,
):
    rows, tokens, width = raw_k.shape
    group = raw_q.shape[0] // rows
    score_slots = (scores_a, scores_b)
    column = lax.broadcasted_iota(jnp.int32, (tile, tokens), 1)
    token = lax.broadcasted_iota(jnp.int32, (tile, tokens), 0)

    def load(r):
        here = rows_of(r, group)
        there = pl.ds(pl.multiple_of((first + r) * group, group), group)
        return pltpu.make_async_copy(queries.at[there], raw_q.at[here], q_sems.at[r])

    keys_in = pltpu.make_async_copy(keys.at[pl.ds(first, rows)], raw_k, key_sem)
    keys_in.start()

    def start(r, carry):
        load(r).start()
        return carry

    lax.fori_loop(0, rows, start, 0)

    def rotate(x):
        x = x.astype(jnp.float32)
        turned = pltpu.roll(x, width // 2, x.ndim - 1)
        return (x * cosine[...] + turned * sine[...]).astype(jnp.bfloat16)

    def score(r, slot):
        load(r).wait()
        span = rows_of(r, group)
        q = rotate(raw_q[span])
        k = rotate(raw_k[r])
        out_q[span] = q
        out_k[r] = k
        score_slots[slot][...] = lax.dot_general(
            q.reshape(group * tokens, width),
            k,
            (((1,), (1,)), ((), ())),
            preferred_element_type=jnp.float32,
        )

    def weigh(r, slot):
        for h in range(group):
            for t in range(0, tokens, tile):
                begin = h * tokens + t
                s = score_slots[slot][begin : begin + tile]
                s = jnp.where(column <= token + t, s, -jnp.inf)
                highest = jnp.max(s, axis=-1, keepdims=True)
                weights = jnp.exp2((s - highest) * exp2_scale)
                out_w[r * group + h, t : t + tile, :] = weights.astype(jnp.bfloat16)
                out_m[r * group + h, t : t + tile, :] = jnp.broadcast_to(highest, (tile, width))

    keys_in.wait()
    score(0, 0)

    def two_rows(step, carry):
        for u in range(2):
            r = step * 2 + u
            score(r + 1, 1 - u)
            weigh(r, u)
        return carry

    pairs = (rows - 1) // 2
    lax.fori_loop(0, pairs, two_rows, 0)
    for r in range(2 * pairs, rows):
        if r + 1 < rows:
            score(r + 1, (r + 1) % 2)
        weigh(r, r % 2)


def prepare(cosine, sine, queries, keys, first, rows, vmem):
    total, tokens, width = keys.shape
    group = queries.shape[0] // total
    in_vmem = pl.BlockSpec(memory_space=pltpu.VMEM)
    in_hbm = pl.BlockSpec(memory_space=pltpu.HBM)
    return pl.pallas_call(
        functools.partial(prepare_kernel, first=first, tile=math.gcd(tokens, 64)),
        out_shape=[
            jax.ShapeDtypeStruct((rows * group, tokens, width), jnp.bfloat16),
            jax.ShapeDtypeStruct((rows, tokens, width), jnp.bfloat16),
            jax.ShapeDtypeStruct((rows * group, tokens, tokens), jnp.bfloat16),
            jax.ShapeDtypeStruct((rows * group, tokens, width), jnp.float32),
        ],
        in_specs=[in_vmem] * 2 + [in_hbm] * 2,
        out_specs=[in_vmem] * 4,
        scratch_shapes=[
            pltpu.VMEM((rows * group, tokens, width), jnp.bfloat16),
            pltpu.VMEM((rows, tokens, width), jnp.bfloat16),
            pltpu.VMEM((group * tokens, tokens), jnp.float32),
            pltpu.VMEM((group * tokens, tokens), jnp.float32),
            pltpu.SemaphoreType.DMA((rows,)),
            pltpu.SemaphoreType.DMA(()),
        ],
        cost_estimate=pl.CostEstimate(
            flops=2 * rows * group * tokens * tokens * width,
            bytes_accessed=2 * rows * (group + 1) * tokens * width,
            transcendentals=rows * group * tokens * tokens,
        ),
        compiler_params=pltpu.CompilerParams(vmem_limit_bytes=vmem),
        name="prepare",
    )(cosine, sine, queries, keys)


def attend_kernel(live, values, prefix, *refs, parts, heads, block, tile):
    prepared = [refs[4 * p : 4 * p + 4] for p in range(parts)]
    out, staged, score_a, score_b, weight_a, weight_b, guard, sems = refs[4 * parts :]
    score_slots, weight_slots = (score_a, score_b), (weight_a, weight_b)
    rows, tokens, width = values.shape
    group = out.shape[0] // rows
    part_rows = rows // parts
    prefix_rows = prefix.shape[0]
    value_base = heads * width
    place = lax.axis_index("grp") * lax.axis_size("seq") + lax.axis_index("seq")
    column = lax.broadcasted_iota(jnp.int32, (tile, tokens), 1)
    token = lax.broadcasted_iota(jnp.int32, (tile, tokens), 0)
    out_token = lax.broadcasted_iota(jnp.int32, (tokens, width), 0)
    guard[...] = jnp.full(guard.shape, -jnp.inf, jnp.float32)

    def prefix_keys(r):
        return prefix[:, pl.ds(pl.multiple_of(lax.rem(r, heads) * width, width), width)]

    def score(part, r, count, slot, own_too):
        queries, keys = prepared[part][0], prepared[part][1]
        here = r - part * part_rows
        q = queries[rows_of(here, group), :count, :].reshape(group * count, width)
        k = prefix_keys(r)
        if own_too:
            k = jnp.concatenate([k, keys[here]], axis=0)
        score_slots[slot][: group * count, : k.shape[0]] = lax.dot_general(
            q, k, (((1,), (1,)), ((), ())), preferred_element_type=jnp.float32
        )

    def across(x):
        if prefix_rows % width:
            return x[:, :1]
        return jnp.concatenate([x] * (prefix_rows // width), axis=1)

    def weigh_prefix(part, r, count, slot):
        own_w, own_m = prepared[part][2], prepared[part][3]
        base = (r - part * part_rows) * group
        worst = jnp.full((8, prefix_rows), -jnp.inf, jnp.float32)
        for h in range(group):
            for t in range(0, count, tile):
                begin = h * count + t
                s = score_slots[slot][begin : begin + tile, :prefix_rows]
                above = (s - across(own_m[base + h, t : t + tile, :])) * exp2_scale
                worst = jnp.maximum(worst, jnp.max(above.reshape(-1, 8, prefix_rows), axis=0))
                weight_slots[slot][begin : begin + tile, :prefix_rows] = jnp.exp2(above).astype(
                    jnp.bfloat16
                )
        guard[...] = jnp.maximum(guard[...], worst)

    def weigh_all(count, slot):
        for begin in range(0, group * count, tile):
            s = score_slots[slot][begin : begin + tile]
            own = jnp.where(column <= token + begin % count, s[:, prefix_rows:], -jnp.inf)
            s = jnp.concatenate([s[:, :prefix_rows], own], axis=1)
            highest = jnp.max(s, axis=-1, keepdims=True)
            weights = jnp.exp2((s - highest) * exp2_scale)
            weight_slots[slot][begin : begin + tile] = weights.astype(jnp.bfloat16)

    def gather_values(part, r, count, length, slot, own_too):
        column_start = pl.multiple_of(value_base + lax.rem(r, heads) * width, width)
        all_values = jnp.concatenate([prefix[:, pl.ds(column_start, width)], values[r]], axis=0)
        all_values = jnp.concatenate([all_values, jnp.ones_like(all_values)], axis=1)
        if own_too:
            weights = weight_slots[slot][: group * count]
        else:
            own = prepared[part][2][rows_of(r - part * part_rows, group), :count, :]
            weights = jnp.concatenate(
                [
                    weight_slots[slot][: group * count, :prefix_rows],
                    own.reshape(group * count, tokens),
                ],
                axis=1,
            )
        summed = jnp.dot(weights, all_values, preferred_element_type=jnp.float32)
        attended = (summed[:, :width] / summed[:, width:]).astype(jnp.bfloat16)
        attended = attended.reshape(group, count, width)
        span = rows_of(r, group)
        visible = (out_token[:count] < length)[None]
        staged[span, :count, :] = jnp.where(visible, attended, jnp.zeros_like(attended))
        if count < tokens:
            staged[span, count:, :] = jnp.zeros((group, tokens - count, width), jnp.bfloat16)
        pltpu.make_async_copy(staged.at[span], out.at[span], sems.at[r]).start()

    def length_of(r):
        return live[lax.div(place * rows + r, KEY_VALUE_HEADS)]

    def block_of_rows(part, base, count, length):
        score(part, base, count, 0, False)
        for u in range(block):
            slot = u % 2
            if u + 1 < block:
                score(part, base + u + 1, count, 1 - slot, False)
            weigh_prefix(part, base + u, count, slot)
            gather_values(part, base + u, count, length, slot, False)

    for part in range(parts):

        def one_block(index, carry, part=part):
            base = part * part_rows + index * block
            length = length_of(base)
            tiles = jnp.clip(lax.div(length + tile - 1, tile), 1, tokens // tile)
            for n in range(1, tokens // tile + 1):
                run = functools.partial(block_of_rows, part, base, n * tile, length)
                pl.when(tiles == n)(run)
            return carry

        lax.fori_loop(0, part_rows // block, one_block, 0)

    def finish(r, carry):
        span = rows_of(r, group)
        pltpu.make_async_copy(staged.at[span], out.at[span], sems.at[r]).wait()
        return carry

    lax.fori_loop(0, rows, finish, 0)

    @pl.when(jnp.max(guard[...]) > overflow_margin)
    def _():
        for part in range(parts):

            def one_row(index, carry, part=part):
                r = part * part_rows + index
                score(part, r, tokens, 0, True)
                weigh_all(tokens, 0)
                gather_values(part, r, tokens, length_of(r), 0, True)
                return carry

            lax.fori_loop(0, part_rows, one_row, 0)
        lax.fori_loop(0, rows, finish, 0)


def attend(lengths, values, prefix, prepared, rows_out, heads):
    rows, tokens, width = values.shape
    group = rows_out // rows
    parts = len(prepared)
    in_vmem = pl.BlockSpec(memory_space=pltpu.VMEM)
    in_smem = pl.BlockSpec(memory_space=pltpu.SMEM)
    wide = (group * tokens, prefix.shape[0] + tokens)
    return pl.pallas_call(
        functools.partial(
            attend_kernel,
            parts=parts,
            heads=heads,
            block=math.gcd(rows // parts, KEY_VALUE_HEADS),
            tile=math.gcd(tokens, 32),
        ),
        out_shape=jax.ShapeDtypeStruct((rows_out, tokens, width), jnp.bfloat16),
        in_specs=[in_smem] + [in_vmem] * (2 + 4 * parts),
        out_specs=pl.BlockSpec(memory_space=pl.ANY),
        scratch_shapes=[pltpu.VMEM((rows_out, tokens, width), jnp.bfloat16)]
        + [pltpu.VMEM(wide, jnp.float32)] * 2
        + [pltpu.VMEM(wide, jnp.bfloat16)] * 2
        + [pltpu.VMEM((8, prefix.shape[0]), jnp.float32), pltpu.SemaphoreType.DMA((rows,))],
        compiler_params=pltpu.CompilerParams(vmem_limit_bytes=attend_vmem),
        name="attend",
    )(lengths, values, prefix, *[x for part in prepared for x in part])


def shards(
    cand_queries,
    candidate_keys,
    candidate_values,
    prefix_rotated_keys,
    prefix_value_matrix,
    lengths,
):
    sequence_count = lax.axis_size("seq")
    grp_count = lax.axis_size("grp")
    key_value_rows, cand_length, _ = candidate_keys.shape
    heads = min(KEY_VALUE_HEADS, key_value_rows)
    prefix_total = prefix_rotated_keys.shape[0] * sequence_count * grp_count
    wanted = (
        np.arange(sequence_count)[:, None] * key_value_rows + np.arange(heads)[None, :]
    ) % KEY_VALUE_HEADS

    def by_target(matrix):
        split = matrix.reshape(matrix.shape[0], KEY_VALUE_HEADS, HEAD_WIDTH)
        picked = jnp.take(split, wanted.reshape(-1), axis=1)
        return picked.reshape(matrix.shape[0], sequence_count, heads * HEAD_WIDTH).transpose(1, 0, 2)

    near_seq = math.gcd(sequence_count, 2)
    near_grp = math.gcd(grp_count, 2)
    far_seq, far_grp = sequence_count // near_seq, grp_count // near_grp

    def moved(block, far_g, near_g, far_s, near_s):
        if not (far_g or near_g or far_s or near_s):
            return block
        pairs = []
        for source in range(grp_count * sequence_count):
            g, s = divmod(source, sequence_count)
            g = (g // near_grp + far_g) % far_grp * near_grp + (g + near_g) % near_grp
            s = (s // near_seq + far_s) % far_seq * near_seq + (s + near_s) % near_seq
            pairs.append((source, g * sequence_count + s))
        return lax.ppermute(block, ("grp", "seq"), pairs)

    cosine, sine = rotation_tables(prefix_total, cand_length)
    parts = math.gcd(key_value_rows, 2)
    part_rows = key_value_rows // parts

    def prepared_part(p, cosine, sine):
        return prepare(
            cosine, sine, cand_queries, candidate_keys, p * part_rows, part_rows, prepare_vmem[p]
        )

    prepared = [prepared_part(0, cosine, sine)]
    if key_value_rows % KEY_VALUE_HEADS == 0:
        spare = prefix_rotated_keys.shape[1]
        zero = jnp.zeros((), jnp.bfloat16)
        block = lax.pad(prefix_rotated_keys, zero, ((0, 0, 0), (0, spare, 0))) + lax.pad(
            prefix_value_matrix, zero, ((0, 0, 0), (spare, 0, 0))
        )
        block = jnp.concatenate([moved(block, 0, 0, d, 0) for d in range(far_seq)], axis=0)
        block, prepared, cosine, sine = lax.optimization_barrier((block, prepared, cosine, sine))
        block = jnp.concatenate(
            [moved(block, e, 0, 0, d) for e in range(far_grp) for d in range(near_seq)], axis=0
        )
        prepared += [prepared_part(p, cosine, sine) for p in range(1, parts)]
        block, prepared = lax.optimization_barrier((block, prepared))
        prefix = jnp.concatenate([moved(block, 0, e, 0, 0) for e in range(near_grp)], axis=0)
    else:
        outgoing = jnp.concatenate(
            [by_target(prefix_rotated_keys), by_target(prefix_value_matrix)], axis=2
        )
        spread = lax.all_to_all(outgoing, "seq", split_axis=0, concat_axis=0, tiled=True)
        spread = spread.reshape(-1, 2 * heads * HEAD_WIDTH)
        prefix = lax.all_gather(spread, "grp", axis=0, tiled=True)
        prepared += [prepared_part(p, cosine, sine) for p in range(1, parts)]
    return attend(lengths, candidate_values, prefix, prepared, cand_queries.shape[0], heads)


def solution(mesh):
    return jax.shard_map(
        shards,
        mesh=mesh,
        in_specs=(
            P(("grp", "seq"), None, None),
            P(("grp", "seq"), None, None),
            P(("grp", "seq"), None, None),
            P(("grp", "seq"), None),
            P(("grp", "seq"), None),
            P(),
        ),
        out_specs=P(("grp", "seq"), None, None),
        check_vma=False,
    )
```

time: 28.8 us -> 38.9 us (1.35)
  the two profiles are of different devices: /device:TPU:1 before, /device:TPU:0 now
where the time goes in v3:
time: 38.9 us; the launch traced here: 38.8 us
  Pallas kernels  24.4 us (63%)
  starting transfers between devices  9.77 us (25%)
  waiting for transfers between devices  1.88 us (5%)
  other arithmetic  1.4 us (4%)
  local copies, waits for them, and re-layouts  1.06 us (3%)
    pallas_call x1, Pallas kernels, attend(): pl.pallas_call(functools.partial(attend_kernel, parts=parts, heads=heads,...  16.8 us
    ppermute x7, starting transfers between devices, moved(): return lax.ppermute(block, ('grp', 'seq'), pairs)  9.77 us
    pallas_call x2, Pallas kernels, prepare(): pl.pallas_call(functools.partial(prepare_kernel, first=first, tile=math.g...  7.59 us
    ppermute x7, waiting for transfers between devices, moved(): return lax.ppermute(block, ('grp', 'seq'), pairs)  1.88 us
    unnamed x10, local copies, waits for them, and re-layouts  1.06 us
    add x1, other arithmetic, shards(): lax.pad(prefix_rotated_keys, zero, ((0, 0, 0), (0, spare, 0)))  0.87 us
  transfers between devices with their start and end apart: 7, of which 2 were waited for; matrix products, arithmetic and copies ran while one was open for 1% of the time, Pallas kernels for 20%

profile of v3, /device:TPU:0, one launch (start us, length us, event | category | flops | bytes accessed | tf_op | source)
XLA Modules:
  0.0 38.8 jit_solution(15554439284408126302)
XLA Ops:
  0.0 0.0 copy-start
  0.0 0.9 %pad_add_fusion = bf16[4,2048]{1,0:T(4,128)(2,1)S(1)} fusion(bf16[4,1024]{1,0:T(4,128)(2,1)} %param.10, bf16[4,1024]{1,0:T(4,128)(2,1)} %param.9), kind=kLoop, calls=%fused_computation.8 | loop fusion | flops 32768 | bytes 32768 | tf_op jit(solution)/shard_map/add | solution.py:365
  0.9 5.1 %collective-permute-start.2 = (bf16[4,2048]{1,0:T(4,128)(2,1)S(1)}, bf16[4,2048]{1,0:T(4,128)(2,1)S(1)}, u32[]{:S(2)}, u32[]{:S(2)}) collective-permute-start(bf16[4,2048]{1,0:T(4,128)(2,1)S(1)} %pad_add_fusion), channel_id=1, source_target_pairs={{0,6},{1,7},{2,0},{3,1},{4,2},{5,3},{6,4},{7,5},{8,14},{9,15},{10,... | collective-permute-start | bytes 49160 | tf_op jit(solution)/shard_map/ppermute | solution.py:350
  6.0 0.0 collective-permute-start.1
  6.0 1.0 %collective-permute-start = (bf16[4,2048]{1,0:T(4,128)(2,1)S(1)}, bf16[4,2048]{1,0:T(4,128)(2,1)S(1)}, u32[]{:S(2)}, u32[]{:S(2)}) collective-permute-start(bf16[4,2048]{1,0:T(4,128)(2,1)S(1)} %pad_add_fusion), channel_id=1, source_target_pairs={{0,2},{1,3},{2,4},{3,5},{4,6},{5,7},{6,0},{7,1},{8,10},{9,11},{10,... | collective-permute-start | bytes 49160 | tf_op jit(solution)/shard_map/ppermute | solution.py:350
  7.0 0.3 fusion
  7.4 0.1 pad_maximum_fusion.3
  7.5 0.0 copy-start.1
  7.5 1.0 %copy-done.1 = bf16[16,128,128]{2,1,0:T(8,128)(2,1)S(1)} copy-done((bf16[16,128,128]{2,1,0:T(8,128)(2,1)S(1)}, bf16[16,128,128]{2,1,0:T(8,128)(2,1)}, u32[]{:S(2)}) %copy-start.1) | copy-done | bytes 524312
  8.5 0.0 copy-start.2
  8.5 4.2 %prepare.2 = (bf16[64,128,128]{2,1,0:T(8,128)(2,1)S(1)}, bf16[8,128,128]{2,1,0:T(8,128)(2,1)S(1)}, bf16[64,128,128]{2,1,0:T(8,128)(2,1)S(1)}, f32[64,128,128]{2,1,0:T(8,128)S(1)}) custom-call(f32[128,128]{1,0:T(8,128)S(1)} %get-tuple-element.38.cosine, f32[128,128]{1,0:T(8,128)S(1)} %get-tuple-element.39.sine, bf16[128,128,128]{2,1,0:T(8,128)(2,1)} %queries.3, ...), custom_call_target="tpu_custom_call" | custom-call | flops 268435456 | bytes 2359296 | tf_op jit(solution)/shard_map/prepare/pallas_call | solution.py:130
  12.7 0.0 copy-start.3
  12.7 0.0 copy-start.4
  12.8 0.0 collective-permute-done.2
  12.8 0.0 collective-permute-done.1
  12.8 0.0 collective-permute-done
  12.8 2.5 %collective-permute-start.5 = (bf16[16,2048]{1,0:T(8,128)(2,1)S(1)}, bf16[16,2048]{1,0:T(8,128)(2,1)S(1)}, u32[]{:S(2)}, u32[]{:S(2)}) collective-permute-start(bf16[16,2048]{1,0:T(8,128)(2,1)S(1)} %pad_maximum_fusion.2), channel_id=1, source_target_pairs={{0,17},{1,16},{2,19},{3,18},{4,21},{5,20},{6,23},{7,22},{8,25},{9,... | collective-permute-start | bytes 196616 | tf_op jit(solution)/shard_map/ppermute | solution.py:350
  15.3 0.5 %collective-permute-start.4 = (bf16[16,2048]{1,0:T(8,128)(2,1)S(1)}, bf16[16,2048]{1,0:T(8,128)(2,1)S(1)}, u32[]{:S(2)}, u32[]{:S(2)}) collective-permute-start(bf16[16,2048]{1,0:T(8,128)(2,1)S(1)} %pad_maximum_fusion.2), channel_id=1, source_target_pairs={{0,16},{1,17},{2,18},{3,19},{4,20},{5,21},{6,22},{7,23},{8,24},{9,... | collective-permute-start | bytes 196616 | tf_op jit(solution)/shard_map/ppermute | solution.py:350
  15.9 0.5 %collective-permute-start.3 = (bf16[16,2048]{1,0:T(8,128)(2,1)S(1)}, bf16[16,2048]{1,0:T(8,128)(2,1)S(1)}, u32[]{:S(2)}, u32[]{:S(2)}) collective-permute-start(bf16[16,2048]{1,0:T(8,128)(2,1)S(1)} %pad_maximum_fusion.2), channel_id=1, source_target_pairs={{0,1},{1,0},{2,3},{3,2},{4,5},{5,4},{6,7},{7,6},{8,9},{9,8},{10,11... | collective-permute-start | bytes 196616 | tf_op jit(solution)/shard_map/ppermute | solution.py:350
  16.4 0.0 copy-done
  16.4 0.0 copy-done.2
  16.4 3.4 %prepare.3 = (bf16[64,128,128]{2,1,0:T(8,128)(2,1)S(1)}, bf16[8,128,128]{2,1,0:T(8,128)(2,1)S(1)}, bf16[64,128,128]{2,1,0:T(8,128)(2,1)S(1)}, f32[64,128,128]{2,1,0:T(8,128)S(1)}) custom-call(f32[128,128]{1,0:T(8,128)S(1)} %get-tuple-element.38.cosine, f32[128,128]{1,0:T(8,128)S(1)} %get-tuple-element.39.sine, bf16[128,128,128]{2,1,0:T(8,128)(2,1)S(1)} %copy-done, ...), custom_call_target="tpu_custom_call" | custom-call | flops 268435456 | bytes 2359296 | tf_op jit(solution)/shard_map/prepare/pallas_call | solution.py:130
  19.8 0.0 collective-permute-done.5
  19.8 0.0 collective-permute-done.4
  19.8 0.3 collective-permute-done.3
  20.2 0.1 collective-permute-start.6
  20.2 1.5 %collective-permute-done.6 = bf16[64,2048]{1,0:T(8,128)(2,1)S(1)} collective-permute-done((bf16[64,2048]{1,0:T(8,128)(2,1)S(1)}, bf16[64,2048]{1,0:T(8,128)(2,1)S(1)}, u32[]{:S(2)}, u32[]{:S(2)}) %collective-permute-start.6) | collective-permute-done | bytes 262176 | tf_op jit(solution)/shard_map/ppermute | solution.py:350
  21.8 0.0 copy-done.3
  21.8 0.0 copy-done.4
  21.8 16.8 %attend.1 = bf16[128,128,128]{2,1,0:T(8,128)(2,1)} custom-call(s32[64]{0:T(128)S(1)} %copy-done.4, bf16[16,128,128]{2,1,0:T(8,128)(2,1)S(1)} %copy-done.3, bf16[128,2048]{1,0:T(8,128)(2,1)S(1)} %pad_maximum_fusion.prefix, bf16[64,128,128]{2,1,0:T(8,128)(2,1)S(1)} %get-tuple-element.45.refs_0_, bf16[8,128,128]{2,1,0:T(8,128)(2,1)S(1)} %get-tuple-element.46.refs_1_, ...), custom_call_target="tpu_custom_call" | custom-call | tf_op jit(solution)/shard_map/attend/pallas_call | solution.py:295
  (5 shorter events, 0.1 us)
Async XLA Ops:
  0.0 16.4 %copy-start = (bf16[128,128,128]{2,1,0:T(8,128)(2,1)S(1)}, bf16[128,128,128]{2,1,0:T(8,128)(2,1)}, u32[]{:S(2)}) copy-start(bf16[128,128,128]{2,1,0:T(8,128)(2,1)} %queries.3) | copy-start | bytes 12582916
  0.9 11.9 %collective-permute-start.2 = (bf16[4,2048]{1,0:T(4,128)(2,1)S(1)}, bf16[4,2048]{1,0:T(4,128)(2,1)S(1)}, u32[]{:S(2)}, u32[]{:S(2)}) collective-permute-start(bf16[4,2048]{1,0:T(4,128)(2,1)S(1)} %pad_add_fusion), channel_id=1, source_target_pairs={{0,6},{1,7},{2,0},{3,1},{4,2},{5,3},{6,4},{7,5},{8,14},{9,15},{10,... | collective-permute-start | bytes 49160 | tf_op jit(solution)/shard_map/ppermute | solution.py:350
  6.0 6.8 %collective-permute-start.1 = (bf16[4,2048]{1,0:T(4,128)(2,1)S(1)}, bf16[4,2048]{1,0:T(4,128)(2,1)S(1)}, u32[]{:S(2)}, u32[]{:S(2)}) collective-permute-start(bf16[4,2048]{1,0:T(4,128)(2,1)S(1)} %pad_add_fusion), channel_id=1, source_target_pairs={{0,4},{1,5},{2,6},{3,7},{4,0},{5,1},{6,2},{7,3},{8,12},{9,13},{10,... | collective-permute-start | bytes 49160 | tf_op jit(solution)/shard_map/ppermute | solution.py:350
  6.0 6.8 %collective-permute-start = (bf16[4,2048]{1,0:T(4,128)(2,1)S(1)}, bf16[4,2048]{1,0:T(4,128)(2,1)S(1)}, u32[]{:S(2)}, u32[]{:S(2)}) collective-permute-start(bf16[4,2048]{1,0:T(4,128)(2,1)S(1)} %pad_add_fusion), channel_id=1, source_target_pairs={{0,2},{1,3},{2,4},{3,5},{4,6},{5,7},{6,0},{7,1},{8,10},{9,11},{10,... | collective-permute-start | bytes 49160 | tf_op jit(solution)/shard_map/ppermute | solution.py:350
  7.5 1.0 %copy-start.1 = (bf16[16,128,128]{2,1,0:T(8,128)(2,1)S(1)}, bf16[16,128,128]{2,1,0:T(8,128)(2,1)}, u32[]{:S(2)}) copy-start(bf16[16,128,128]{2,1,0:T(8,128)(2,1)} %keys.3) | copy-start | bytes 1572868
  8.5 7.9 %copy-start.2 = (bf16[16,128,128]{2,1,0:T(8,128)(2,1)S(1)}, bf16[16,128,128]{2,1,0:T(8,128)(2,1)}, u32[]{:S(2)}) copy-start(bf16[16,128,128]{2,1,0:T(8,128)(2,1)} %keys.3) | copy-start | bytes 1572868
  12.7 9.1 %copy-start.3 = (bf16[16,128,128]{2,1,0:T(8,128)(2,1)S(1)}, bf16[16,128,128]{2,1,0:T(8,128)(2,1)}, u32[]{:S(2)}) copy-start(bf16[16,128,128]{2,1,0:T(8,128)(2,1)} %values.1) | copy-start | bytes 1572868
  12.7 9.1 %copy-start.4 = (s32[64]{0:T(128)S(1)}, s32[64]{0:T(128)}, u32[]{:S(2)}) copy-start(s32[64]{0:T(128)} %live.1) | copy-start | bytes 772
  12.8 7.0 %collective-permute-start.5 = (bf16[16,2048]{1,0:T(8,128)(2,1)S(1)}, bf16[16,2048]{1,0:T(8,128)(2,1)S(1)}, u32[]{:S(2)}, u32[]{:S(2)}) collective-permute-start(bf16[16,2048]{1,0:T(8,128)(2,1)S(1)} %pad_maximum_fusion.2), channel_id=1, source_target_pairs={{0,17},{1,16},{2,19},{3,18},{4,21},{5,20},{6,23},{7,22},{8,25},{9,... | collective-permute-start | bytes 196616 | tf_op jit(solution)/shard_map/ppermute | solution.py:350
  15.3 4.5 %collective-permute-start.4 = (bf16[16,2048]{1,0:T(8,128)(2,1)S(1)}, bf16[16,2048]{1,0:T(8,128)(2,1)S(1)}, u32[]{:S(2)}, u32[]{:S(2)}) collective-permute-start(bf16[16,2048]{1,0:T(8,128)(2,1)S(1)} %pad_maximum_fusion.2), channel_id=1, source_target_pairs={{0,16},{1,17},{2,18},{3,19},{4,20},{5,21},{6,22},{7,23},{8,24},{9,... | collective-permute-start | bytes 196616 | tf_op jit(solution)/shard_map/ppermute | solution.py:350
  15.9 4.3 %collective-permute-start.3 = (bf16[16,2048]{1,0:T(8,128)(2,1)S(1)}, bf16[16,2048]{1,0:T(8,128)(2,1)S(1)}, u32[]{:S(2)}, u32[]{:S(2)}) collective-permute-start(bf16[16,2048]{1,0:T(8,128)(2,1)S(1)} %pad_maximum_fusion.2), channel_id=1, source_target_pairs={{0,1},{1,0},{2,3},{3,2},{4,5},{5,4},{6,7},{7,6},{8,9},{9,8},{10,11... | collective-permute-start | bytes 196616 | tf_op jit(solution)/shard_map/ppermute | solution.py:350
  20.2 1.6 %collective-permute-start.6 = (bf16[64,2048]{1,0:T(8,128)(2,1)S(1)}, bf16[64,2048]{1,0:T(8,128)(2,1)S(1)}, u32[]{:S(2)}, u32[]{:S(2)}) collective-permute-start(bf16[64,2048]{1,0:T(8,128)(2,1)S(1)} %pad_maximum_fusion.1), channel_id=1, source_target_pairs={{0,8},{1,9},{2,10},{3,11},{4,12},{5,13},{6,14},{7,15},{8,0},{9,1},... | collective-permute-start | bytes 786440 | tf_op jit(solution)/shard_map/ppermute | solution.py:350

commit v4 on v3

--- a/solution.py
+++ b/solution.py
@@ -128,7 +128,7 @@
     in_vmem = pl.BlockSpec(memory_space=pltpu.VMEM)
     in_hbm = pl.BlockSpec(memory_space=pltpu.HBM)
     return pl.pallas_call(
-        functools.partial(prepare_kernel, first=first, tile=math.gcd(tokens, 64)),
+        functools.partial(prepare_kernel, first=first, tile=math.gcd(tokens, 128)),
         out_shape=[
             jax.ShapeDtypeStruct((rows * group, tokens, width), jnp.bfloat16),
             jax.ShapeDtypeStruct((rows, tokens, width), jnp.bfloat16),

time: 38.9 us -> 38.9 us (level); the launches traced: 38.8 us -> 38.3 us
  Pallas kernels: 24.4 us -> 23.9 us
    pallas_call x1, Pallas kernels: 16.8 us -> 16.4 us  [attend(): pl.pallas_call(functools.partial(attend_kernel, parts=parts, heads=heads,...]
where the time goes in v4:
time: 38.9 us; the launch traced here: 38.3 us
  Pallas kernels  23.9 us (61%)
  starting transfers between devices  9.77 us (25%)
  waiting for transfers between devices  1.88 us (5%)
  other arithmetic  1.4 us (4%)
  local copies, waits for them, and re-layouts  1.06 us (3%)
    pallas_call x1, Pallas kernels, attend(): pl.pallas_call(functools.partial(attend_kernel, parts=parts, heads=heads,...  16.4 us
    ppermute x7, starting transfers between devices, moved(): return lax.ppermute(block, ('grp', 'seq'), pairs)  9.77 us
    pallas_call x2, Pallas kernels, prepare(): pl.pallas_call(functools.partial(prepare_kernel, first=first, tile=math.g...  7.57 us
    ppermute x7, waiting for transfers between devices, moved(): return lax.ppermute(block, ('grp', 'seq'), pairs)  1.88 us
    unnamed x10, local copies, waits for them, and re-layouts  1.06 us
    add x1, other arithmetic, shards(): lax.pad(prefix_rotated_keys, zero, ((0, 0, 0), (0, spare, 0)))  0.87 us
  transfers between devices with their start and end apart: 7, of which 2 were waited for; matrix products, arithmetic and copies ran while one was open for 1% of the time, Pallas kernels for 20%

profile of v4, /device:TPU:0, one launch (start us, length us, event | category | flops | bytes accessed | tf_op | source)
XLA Modules:
  0.0 38.3 jit_solution(3401694570145783004)
XLA Ops:
  0.0 0.0 copy-start
  0.0 0.9 %pad_add_fusion = bf16[4,2048]{1,0:T(4,128)(2,1)S(1)} fusion(bf16[4,1024]{1,0:T(4,128)(2,1)} %param.10, bf16[4,1024]{1,0:T(4,128)(2,1)} %param.9), kind=kLoop, calls=%fused_computation.8 | loop fusion | flops 32768 | bytes 32768 | tf_op jit(solution)/shard_map/add | solution.py:365
  0.9 5.1 %collective-permute-start.2 = (bf16[4,2048]{1,0:T(4,128)(2,1)S(1)}, bf16[4,2048]{1,0:T(4,128)(2,1)S(1)}, u32[]{:S(2)}, u32[]{:S(2)}) collective-permute-start(bf16[4,2048]{1,0:T(4,128)(2,1)S(1)} %pad_add_fusion), channel_id=1, source_target_pairs={{0,6},{1,7},{2,0},{3,1},{4,2},{5,3},{6,4},{7,5},{8,14},{9,15},{10,... | collective-permute-start | bytes 49160 | tf_op jit(solution)/shard_map/ppermute | solution.py:350
  6.0 0.0 collective-permute-start.1
  6.0 1.0 %collective-permute-start = (bf16[4,2048]{1,0:T(4,128)(2,1)S(1)}, bf16[4,2048]{1,0:T(4,128)(2,1)S(1)}, u32[]{:S(2)}, u32[]{:S(2)}) collective-permute-start(bf16[4,2048]{1,0:T(4,128)(2,1)S(1)} %pad_add_fusion), channel_id=1, source_target_pairs={{0,2},{1,3},{2,4},{3,5},{4,6},{5,7},{6,0},{7,1},{8,10},{9,11},{10,... | collective-permute-start | bytes 49160 | tf_op jit(solution)/shard_map/ppermute | solution.py:350
  7.0 0.3 fusion
  7.4 0.1 pad_maximum_fusion.3
  7.5 0.0 copy-start.1
  7.5 1.0 %copy-done.1 = bf16[16,128,128]{2,1,0:T(8,128)(2,1)S(1)} copy-done((bf16[16,128,128]{2,1,0:T(8,128)(2,1)S(1)}, bf16[16,128,128]{2,1,0:T(8,128)(2,1)}, u32[]{:S(2)}) %copy-start.1) | copy-done | bytes 524312
  8.5 0.0 copy-start.2
  8.5 4.2 %prepare.2 = (bf16[64,128,128]{2,1,0:T(8,128)(2,1)S(1)}, bf16[8,128,128]{2,1,0:T(8,128)(2,1)S(1)}, bf16[64,128,128]{2,1,0:T(8,128)(2,1)S(1)}, f32[64,128,128]{2,1,0:T(8,128)S(1)}) custom-call(f32[128,128]{1,0:T(8,128)S(1)} %get-tuple-element.38.cosine, f32[128,128]{1,0:T(8,128)S(1)} %get-tuple-element.39.sine, bf16[128,128,128]{2,1,0:T(8,128)(2,1)} %queries.3, ...), custom_call_target="tpu_custom_call" | custom-call | flops 268435456 | bytes 2359296 | tf_op jit(solution)/shard_map/prepare/pallas_call | solution.py:130
  12.7 0.0 copy-start.3
  12.7 0.0 copy-start.4
  12.7 0.0 collective-permute-done.2
  12.8 0.0 collective-permute-done.1
  12.8 0.0 collective-permute-done
  12.8 2.5 %collective-permute-start.5 = (bf16[16,2048]{1,0:T(8,128)(2,1)S(1)}, bf16[16,2048]{1,0:T(8,128)(2,1)S(1)}, u32[]{:S(2)}, u32[]{:S(2)}) collective-permute-start(bf16[16,2048]{1,0:T(8,128)(2,1)S(1)} %pad_maximum_fusion.2), channel_id=1, source_target_pairs={{0,17},{1,16},{2,19},{3,18},{4,21},{5,20},{6,23},{7,22},{8,25},{9,... | collective-permute-start | bytes 196616 | tf_op jit(solution)/shard_map/ppermute | solution.py:350
  15.3 0.5 %collective-permute-start.4 = (bf16[16,2048]{1,0:T(8,128)(2,1)S(1)}, bf16[16,2048]{1,0:T(8,128)(2,1)S(1)}, u32[]{:S(2)}, u32[]{:S(2)}) collective-permute-start(bf16[16,2048]{1,0:T(8,128)(2,1)S(1)} %pad_maximum_fusion.2), channel_id=1, source_target_pairs={{0,16},{1,17},{2,18},{3,19},{4,20},{5,21},{6,22},{7,23},{8,24},{9,... | collective-permute-start | bytes 196616 | tf_op jit(solution)/shard_map/ppermute | solution.py:350
  15.9 0.5 %collective-permute-start.3 = (bf16[16,2048]{1,0:T(8,128)(2,1)S(1)}, bf16[16,2048]{1,0:T(8,128)(2,1)S(1)}, u32[]{:S(2)}, u32[]{:S(2)}) collective-permute-start(bf16[16,2048]{1,0:T(8,128)(2,1)S(1)} %pad_maximum_fusion.2), channel_id=1, source_target_pairs={{0,1},{1,0},{2,3},{3,2},{4,5},{5,4},{6,7},{7,6},{8,9},{9,8},{10,11... | collective-permute-start | bytes 196616 | tf_op jit(solution)/shard_map/ppermute | solution.py:350
  16.4 0.0 copy-done
  16.4 0.0 copy-done.2
  16.4 3.4 %prepare.3 = (bf16[64,128,128]{2,1,0:T(8,128)(2,1)S(1)}, bf16[8,128,128]{2,1,0:T(8,128)(2,1)S(1)}, bf16[64,128,128]{2,1,0:T(8,128)(2,1)S(1)}, f32[64,128,128]{2,1,0:T(8,128)S(1)}) custom-call(f32[128,128]{1,0:T(8,128)S(1)} %get-tuple-element.38.cosine, f32[128,128]{1,0:T(8,128)S(1)} %get-tuple-element.39.sine, bf16[128,128,128]{2,1,0:T(8,128)(2,1)S(1)} %copy-done, ...), custom_call_target="tpu_custom_call" | custom-call | flops 268435456 | bytes 2359296 | tf_op jit(solution)/shard_map/prepare/pallas_call | solution.py:130
  19.8 0.0 collective-permute-done.5
  19.8 0.0 collective-permute-done.4
  19.8 0.3 collective-permute-done.3
  20.2 0.1 collective-permute-start.6
  20.2 1.5 %collective-permute-done.6 = bf16[64,2048]{1,0:T(8,128)(2,1)S(1)} collective-permute-done((bf16[64,2048]{1,0:T(8,128)(2,1)S(1)}, bf16[64,2048]{1,0:T(8,128)(2,1)S(1)}, u32[]{:S(2)}, u32[]{:S(2)}) %collective-permute-start.6) | collective-permute-done | bytes 262176 | tf_op jit(solution)/shard_map/ppermute | solution.py:350
  21.8 0.0 copy-done.3
  21.8 0.0 copy-done.4
  21.8 16.4 %attend.1 = bf16[128,128,128]{2,1,0:T(8,128)(2,1)} custom-call(s32[64]{0:T(128)S(1)} %copy-done.4, bf16[16,128,128]{2,1,0:T(8,128)(2,1)S(1)} %copy-done.3, bf16[128,2048]{1,0:T(8,128)(2,1)S(1)} %pad_maximum_fusion.prefix, bf16[64,128,128]{2,1,0:T(8,128)(2,1)S(1)} %get-tuple-element.45.refs_0_, bf16[8,128,128]{2,1,0:T(8,128)(2,1)S(1)} %get-tuple-element.46.refs_1_, ...), custom_call_target="tpu_custom_call" | custom-call | tf_op jit(solution)/shard_map/attend/pallas_call | solution.py:295
  (5 shorter events, 0.1 us)
Async XLA Ops:
  0.0 16.4 %copy-start = (bf16[128,128,128]{2,1,0:T(8,128)(2,1)S(1)}, bf16[128,128,128]{2,1,0:T(8,128)(2,1)}, u32[]{:S(2)}) copy-start(bf16[128,128,128]{2,1,0:T(8,128)(2,1)} %queries.3) | copy-start | bytes 12582916
  0.9 11.9 %collective-permute-start.2 = (bf16[4,2048]{1,0:T(4,128)(2,1)S(1)}, bf16[4,2048]{1,0:T(4,128)(2,1)S(1)}, u32[]{:S(2)}, u32[]{:S(2)}) collective-permute-start(bf16[4,2048]{1,0:T(4,128)(2,1)S(1)} %pad_add_fusion), channel_id=1, source_target_pairs={{0,6},{1,7},{2,0},{3,1},{4,2},{5,3},{6,4},{7,5},{8,14},{9,15},{10,... | collective-permute-start | bytes 49160 | tf_op jit(solution)/shard_map/ppermute | solution.py:350
  6.0 6.7 %collective-permute-start.1 = (bf16[4,2048]{1,0:T(4,128)(2,1)S(1)}, bf16[4,2048]{1,0:T(4,128)(2,1)S(1)}, u32[]{:S(2)}, u32[]{:S(2)}) collective-permute-start(bf16[4,2048]{1,0:T(4,128)(2,1)S(1)} %pad_add_fusion), channel_id=1, source_target_pairs={{0,4},{1,5},{2,6},{3,7},{4,0},{5,1},{6,2},{7,3},{8,12},{9,13},{10,... | collective-permute-start | bytes 49160 | tf_op jit(solution)/shard_map/ppermute | solution.py:350
  6.0 6.8 %collective-permute-start = (bf16[4,2048]{1,0:T(4,128)(2,1)S(1)}, bf16[4,2048]{1,0:T(4,128)(2,1)S(1)}, u32[]{:S(2)}, u32[]{:S(2)}) collective-permute-start(bf16[4,2048]{1,0:T(4,128)(2,1)S(1)} %pad_add_fusion), channel_id=1, source_target_pairs={{0,2},{1,3},{2,4},{3,5},{4,6},{5,7},{6,0},{7,1},{8,10},{9,11},{10,... | collective-permute-start | bytes 49160 | tf_op jit(solution)/shard_map/ppermute | solution.py:350
  7.5 1.0 %copy-start.1 = (bf16[16,128,128]{2,1,0:T(8,128)(2,1)S(1)}, bf16[16,128,128]{2,1,0:T(8,128)(2,1)}, u32[]{:S(2)}) copy-start(bf16[16,128,128]{2,1,0:T(8,128)(2,1)} %keys.3) | copy-start | bytes 1572868
  8.5 7.9 %copy-start.2 = (bf16[16,128,128]{2,1,0:T(8,128)(2,1)S(1)}, bf16[16,128,128]{2,1,0:T(8,128)(2,1)}, u32[]{:S(2)}) copy-start(bf16[16,128,128]{2,1,0:T(8,128)(2,1)} %keys.3) | copy-start | bytes 1572868
  12.7 9.1 %copy-start.3 = (bf16[16,128,128]{2,1,0:T(8,128)(2,1)S(1)}, bf16[16,128,128]{2,1,0:T(8,128)(2,1)}, u32[]{:S(2)}) copy-start(bf16[16,128,128]{2,1,0:T(8,128)(2,1)} %values.1) | copy-start | bytes 1572868
  12.7 9.1 %copy-start.4 = (s32[64]{0:T(128)S(1)}, s32[64]{0:T(128)}, u32[]{:S(2)}) copy-start(s32[64]{0:T(128)} %live.1) | copy-start | bytes 772
  12.8 7.0 %collective-permute-start.5 = (bf16[16,2048]{1,0:T(8,128)(2,1)S(1)}, bf16[16,2048]{1,0:T(8,128)(2,1)S(1)}, u32[]{:S(2)}, u32[]{:S(2)}) collective-permute-start(bf16[16,2048]{1,0:T(8,128)(2,1)S(1)} %pad_maximum_fusion.2), channel_id=1, source_target_pairs={{0,17},{1,16},{2,19},{3,18},{4,21},{5,20},{6,23},{7,22},{8,25},{9,... | collective-permute-start | bytes 196616 | tf_op jit(solution)/shard_map/ppermute | solution.py:350
  15.3 4.4 %collective-permute-start.4 = (bf16[16,2048]{1,0:T(8,128)(2,1)S(1)}, bf16[16,2048]{1,0:T(8,128)(2,1)S(1)}, u32[]{:S(2)}, u32[]{:S(2)}) collective-permute-start(bf16[16,2048]{1,0:T(8,128)(2,1)S(1)} %pad_maximum_fusion.2), channel_id=1, source_target_pairs={{0,16},{1,17},{2,18},{3,19},{4,20},{5,21},{6,22},{7,23},{8,24},{9,... | collective-permute-start | bytes 196616 | tf_op jit(solution)/shard_map/ppermute | solution.py:350
  15.9 4.3 %collective-permute-start.3 = (bf16[16,2048]{1,0:T(8,128)(2,1)S(1)}, bf16[16,2048]{1,0:T(8,128)(2,1)S(1)}, u32[]{:S(2)}, u32[]{:S(2)}) collective-permute-start(bf16[16,2048]{1,0:T(8,128)(2,1)S(1)} %pad_maximum_fusion.2), channel_id=1, source_target_pairs={{0,1},{1,0},{2,3},{3,2},{4,5},{5,4},{6,7},{7,6},{8,9},{9,8},{10,11... | collective-permute-start | bytes 196616 | tf_op jit(solution)/shard_map/ppermute | solution.py:350
  20.2 1.6 %collective-permute-start.6 = (bf16[64,2048]{1,0:T(8,128)(2,1)S(1)}, bf16[64,2048]{1,0:T(8,128)(2,1)S(1)}, u32[]{:S(2)}, u32[]{:S(2)}) collective-permute-start(bf16[64,2048]{1,0:T(8,128)(2,1)S(1)} %pad_maximum_fusion.1), channel_id=1, source_target_pairs={{0,8},{1,9},{2,10},{3,11},{4,12},{5,13},{6,14},{7,15},{8,0},{9,1},... | collective-permute-start | bytes 786440 | tf_op jit(solution)/shard_map/ppermute | solution.py:350
